TPU v7x, 32 devices: a whole 2x2x4 slice. The times are simulated.
32 devices in a mesh: sec: 8 (over z, x), tile: 4 (over y, core).
Axes of the slice: x: 2, y: 2, z: 4, core: 2. Of those that a mesh axis runs over, the one named last changes fastest.
Arguments:
- displacement: float32 [2, 8, 1024, 2048], P(None, 'sec', 'tile'), may hold values from -6 to 6
- spring: float32 [8, 1024, 2048], P('sec', 'tile'), may hold values from 0.5 to 2
- stiff_table: float32 [8], replicated, may hold values from 0.25 to 2
- match_blocks: int32 [2, 8, 1024], P(None, 'sec', 'tile'), may hold values from 0 to 4095
- match_class: int32 [8, 1024], P('sec', 'tile'), may hold values from 0 to 7
Outputs:
- relaxed: float32 [2, 8, 1024, 2048], P(None, 'sec', 'tile')
All inputs are finite; a program needn't handle non-finite values.
Results may differ from a plain program's by a relative error of at most 0.000053.
Values sent between devices are 32-bit elements; how exact they have to be, the bound alone decides.
No kernel may reach another device: no remote copies, remote signals or barrier semaphores. Data moves between devices by JAX's collectives and lax.ppermute only.
A program may use at most 128 MiB of HBM per device.

v0:
```python
import functools
import jax
import jax.numpy as jnp
from jax import lax
from jax.experimental import pallas as pl
from jax.experimental.pallas import tpu as pltpu
from jax.sharding import PartitionSpec as P

ITERS = 3
LANES = 128
SUB = 8

VM = pl.BlockSpec(memory_space=pltpu.VMEM)
SM = pl.BlockSpec(memory_space=pltpu.SMEM)
HBM = pl.BlockSpec(memory_space=pltpu.MemorySpace.HBM)


def f32(*shape):
    return jax.ShapeDtypeStruct(shape, jnp.float32)


def tile_row(block, chunks):
    row = block // chunks
    return (row // SUB) * (SUB * chunks) + (block % chunks) * SUB + row % SUB


def pieces(x):
    high = x.astype(jnp.bfloat16)
    low = (x - high.astype(jnp.float32)).astype(jnp.bfloat16)
    return high, low


def summed(same, x):
    high, low = pieces(x)
    return jnp.dot(same, high, preferred_element_type=jnp.float32) + jnp.dot(
        same, low, preferred_element_type=jnp.float32
    )


def parity(axis):
    return lax.axis_index(axis) % 2


def send_edges(entry, halo_a, halo_b, count, chunks):
    odd_tile = parity("tile")
    low = pl.multiple_of(count + (1 - odd_tile) * chunks, SUB)
    high = pl.multiple_of(count + odd_tile * chunks, SUB)
    halo_a[...] = entry[:, pl.ds(low, chunks), :]
    halo_b[...] = entry[:, pl.ds(high, chunks), :]


def levels(classes, table, alive):
    out = jnp.zeros(classes.shape, jnp.float32)
    for level in range(table.shape[0]):
        out = jnp.where(classes == level, table[level], out)
    return out * alive.astype(jnp.float32)


def columns(line):
    return jnp.concatenate(
        [
            jnp.broadcast_to(line[:, at : at + LANES], (LANES, LANES)).T
            for at in range(0, line.shape[1], LANES)
        ],
        axis=0,
    )


def each_slot(count, rows, body):
    def some(step, carry):
        for inner in range(8):
            slot = step * 8 + inner
            body(slot, rows(slot))
        return carry

    lax.fori_loop(0, count // 8, some, 0)


def own_kernel(own, table, classes, displacement, field, entry, stiff, line, level, classes_in, sem):
    copies = [
        pltpu.make_async_copy(displacement, field, sem.at[0]),
        pltpu.make_async_copy(table, level, sem.at[1]),
        pltpu.make_async_copy(classes, classes_in, sem.at[2]),
    ]
    for copy in copies:
        copy.start()
    copies[1].wait()
    copies[2].wait()
    alive = lax.axis_index("sec") < lax.axis_size("sec") - 1
    line[...] = levels(classes_in[...], level, alive)
    stiff[...] = columns(line[...])
    copies[0].wait()

    def take(slot, row):
        for part in range(2):
            entry[part, pl.ds(slot, 1), :] = field[part, pl.ds(row, 1), :]

    each_slot(own.shape[1], lambda j: own[0, j], take)


def first_kernel(chunks, prev, prev_line, own_line, table, field, own_entry, own_stiff, own_stiff_line, entry, stiff, rows, stiff_line, send_x, send_z, halo_a, halo_b):
    blocks = field.shape[1]
    matches = own_entry.shape[1]
    count = 2 * matches
    odd = parity("sec")
    own_at = pl.multiple_of(odd * matches, LANES)
    prev_at = pl.multiple_of((1 - odd) * matches, LANES)

    def take(slot, row):
        for part in range(2):
            entry[part, pl.ds(prev_at + slot, 1), :] = field[part, pl.ds(row, 1), :]

    each_slot(matches, lambda j: prev[0, j], take)
    line = levels(prev_line[1:2, :], table, lax.axis_index("sec") > 0)
    stiff[pl.ds(prev_at, matches), :] = columns(line)
    stiff[pl.ds(own_at, matches), :] = own_stiff[...]
    entry[:, pl.ds(own_at, matches), :] = own_entry[...]
    even = odd == 0
    for out, first, second in ((rows, own_line[...], prev_line[0:1, :]), (stiff_line, own_stiff_line[...], line)):
        out[:, :matches] = jnp.where(even, first, second)
        out[:, matches:] = jnp.where(even, second, first)
    for part in range(2):
        for chunk in range(chunks):
            entry[part, pl.ds(count + chunk, 1), :] = field[part, pl.ds(chunk * SUB, 1), :]
            entry[part, pl.ds(count + chunks + chunk, 1), :] = field[
                part, pl.ds(blocks - SUB * chunks + chunk * SUB + SUB - 1, 1), :
            ]
        send_x[part] = entry[part, :matches, :] * stiff[:matches, :]
        send_z[part] = entry[part, matches:count, :] * stiff[matches:, :]
    send_edges(entry, halo_a, halo_b, count, chunks)


def setup_kernel(chunks, rows, rows_line, stiff_line, spring, same, weight, factor, held, picked, column, sem):
    blocks = held.shape[0]
    count = rows_line.shape[1]
    total = count + 2 * chunks
    copy = pltpu.make_async_copy(spring, held, sem)
    copy.start()
    line = rows_line[...].astype(jnp.float32)
    column[:count, :] = columns(line)
    edge = lax.broadcasted_iota(jnp.int32, (chunks, LANES), 0) * SUB
    column[count : count + chunks, :] = edge.astype(jnp.float32)
    column[count + chunks :, :] = (edge + (blocks - SUB * chunks + SUB - 1)).astype(jnp.float32)

    def band(step, carry):
        at = pl.ds(pl.multiple_of(step * 32, 32), 32)
        col = column[at, :]
        total_stiff = jnp.zeros((32, LANES), jnp.float32)
        for piece in range(count // LANES):
            cut = slice(piece * LANES, (piece + 1) * LANES)
            equal = col == rows_line[:, cut].astype(jnp.float32)
            same[at, cut] = equal.astype(jnp.float32).astype(jnp.bfloat16)
            total_stiff += jnp.where(equal, stiff_line[:, cut], 0.0)
        factor[at, :] = jnp.broadcast_to(jnp.sum(total_stiff, axis=1, keepdims=True), (32, LANES))
        return carry

    lax.fori_loop(0, total // 32, band, 0)
    copy.wait()

    def take(slot, row):
        picked[pl.ds(slot, 1), :] = held[pl.ds(row, 1), :]

    each_slot(count, lambda j: rows[0, j], take)
    for chunk in range(chunks):
        take(count + chunk, chunk * SUB)
        take(count + chunks + chunk, blocks - SUB * chunks + chunk * SUB + SUB - 1)
    spring_here = picked[...]
    inverse = 1.0 / (4.0 * spring_here + factor[...])
    weight[...] = 4.0 * spring_here * inverse
    factor[...] = 0.8 * inverse


def stencil(field, nearby, start, chunks, above=None, below=None):
    span = SUB * chunks
    lane = lax.broadcasted_iota(jnp.int32, (SUB, LANES), 1)
    sub = lax.broadcasted_iota(jnp.int32, (SUB, LANES), 0)
    for part in range(2):

        def at(offset):
            return field[part, pl.ds(start + offset, SUB), :]

        def edge(halo, chunk):
            return jnp.broadcast_to(halo[part][chunk : chunk + 1, :], (SUB, LANES))

        before = jnp.zeros((SUB, LANES), jnp.float32)
        here = at(0)
        for chunk in range(chunks):
            offset = chunk * SUB
            after = at(offset + SUB) if chunk < chunks - 1 else jnp.zeros((SUB, LANES), jnp.float32)
            if above is None:
                up = jnp.where(sub == 0, at(offset - span + SUB - 1), at(offset - 1))
            else:
                up = jnp.where(sub == 0, edge(above, chunk), pltpu.roll(here, 1, 0))
            if below is None:
                down = jnp.where(sub == SUB - 1, at(offset + span - SUB + 1), at(offset + 1))
            else:
                down = jnp.where(sub == SUB - 1, edge(below, chunk), pltpu.roll(here, SUB - 1, 0))
            left = pltpu.roll(jnp.where(lane == LANES - 1, before, here), 1, 1)
            right = pltpu.roll(jnp.where(lane == 0, after, here), LANES - 1, 1)
            nearby[part, pl.ds(start + offset, SUB), :] = 0.2 * (((up + down) + (left + right)) + here)
            before, here = here, after


def inner_strips(field, nearby, chunks):
    span = SUB * chunks
    strips = field.shape[1] // span

    def pair(step, carry):
        for inner in range(2):
            stencil(field, nearby, pl.multiple_of((1 + step * 2 + inner) * span, SUB), chunks)
        return carry

    lax.fori_loop(0, (strips - 2) // 2, pair, 0)


def inner_kernel(chunks, field, nearby):
    inner_strips(field, nearby, chunks)


def scatter_inner_kernel(chunks, rows, entry, stale, field, nearby):
    def put(slot, row):
        for part in range(2):
            field[part, pl.ds(row, 1), :] = entry[part, pl.ds(slot, 1), :]

    each_slot(rows.shape[1], lambda j: rows[0, j], put)
    inner_strips(field, nearby, chunks)


def edge_kernel(chunks, rows, field, entry, got_a, got_b, same, stiff, weight, factor, partial, nearby, base):
    blocks = field.shape[1]
    span = SUB * chunks
    count = rows.shape[1]
    odd_tile = parity("tile") == 1
    above = [jnp.where(odd_tile, got_a[part], got_b[part]) for part in range(2)]
    below = [jnp.where(odd_tile, got_b[part], got_a[part]) for part in range(2)]
    stencil(field, nearby, 0, chunks, above=above)
    stencil(field, nearby, blocks - span, chunks, below=below)

    def take(slot, row):
        for part in range(2):
            base[part, pl.ds(slot, 1), :] = nearby[part, pl.ds(row, 1), :]

    each_slot(count, lambda j: rows[0, j], take)
    for chunk in range(chunks):
        take(count + chunk, chunk * SUB)
        take(count + chunks + chunk, blocks - span + chunk * SUB + SUB - 1)
    own = jnp.concatenate([entry[part, :count, :] * stiff[...] for part in range(2)], axis=1)
    total = summed(same[...], own)
    for part in range(2):
        value = entry[part]
        base[part] = (
            value
            + weight[...] * (base[part] - value)
            - factor[...] * total[:, part * LANES : (part + 1) * LANES]
        )


def new_entries(got_x, got_z, base, same, factor):
    got = jnp.concatenate(
        [jnp.concatenate([got_x[part], got_z[part]], axis=0) for part in range(2)], axis=1
    )
    total = summed(same[...], got)
    return [base[part] + factor[...] * total[:, part * LANES : (part + 1) * LANES] for part in range(2)]


def step_kernel(chunks, got_x, got_z, base, same, factor, stiff, entry, send_x, send_z, halo_a, halo_b):
    matches = got_x.shape[1]
    count = 2 * matches
    for part, value in enumerate(new_entries(got_x, got_z, base, same, factor)):
        entry[part] = value
        send_x[part] = value[:matches] * stiff[:matches, :]
        send_z[part] = value[matches:count] * stiff[matches:, :]
    send_edges(entry, halo_a, halo_b, count, chunks)


def last_kernel(rows, stale, got_x, got_z, base, same, factor, nearby, out, entry, sem):
    for part, value in enumerate(new_entries(got_x, got_z, base, same, factor)):
        entry[part] = value
    stores = []
    for part in range(2):

        def put(slot, row):
            nearby[part, pl.ds(row, 1), :] = entry[part, pl.ds(slot, 1), :]

        each_slot(rows.shape[1], lambda j: rows[0, j], put)
        stores.append(pltpu.make_async_copy(nearby.at[part], out.at[part], sem.at[part]))
        stores[-1].start()
    for copy in stores:
        copy.wait()


def exchange(array, axis, pairs):
    return lax.ppermute(array, axis, pairs)


def pairs_from(first, size):
    out = []
    for i in range(first, size - 1, 2):
        out += [(i, i + 1), (i + 1, i)]
    return out


def on_device(displacement, spring, stiff_table, match_blocks, match_class):
    fields, single, height, breadth = displacement.shape
    chunks = breadth // LANES
    blocks = height * chunks
    matches = match_blocks.shape[2]
    count = 2 * matches
    total = count + 2 * chunks
    sections, tiles = lax.axis_size("sec"), lax.axis_size("tile")
    near, far = pairs_from(0, sections), pairs_from(1, sections)
    near_tile, far_tile = pairs_from(0, tiles), pairs_from(1, tiles)

    def tiled(x):
        lead = x.shape[:-2]
        x = x.reshape(lead + (height // SUB, SUB, chunks, LANES))
        return jnp.swapaxes(x, -3, -2).reshape(lead + (blocks, LANES))

    def untiled(x):
        lead = x.shape[:-2]
        x = x.reshape(lead + (height // SUB, chunks, SUB, LANES))
        return jnp.swapaxes(x, -3, -2).reshape(lead + (height, breadth))

    def call(name, kernel, ins, outs, **more):
        return pl.pallas_call(
            kernel,
            in_specs=ins,
            out_specs=tuple(spec for spec, _ in outs),
            out_shape=tuple(shape for _, shape in outs),
            compiler_params=pltpu.CompilerParams(vmem_limit_bytes=24 << 20),
            name=name,
            **more,
        )

    halo = (VM, f32(fields, chunks, LANES))
    send = (VM, f32(fields, matches, LANES))
    entries = (VM, f32(fields, total, LANES))
    big = (VM, f32(fields, blocks, LANES))
    wide = (VM, f32(total, LANES))
    rows_shape = (VM, jax.ShapeDtypeStruct((1, count), jnp.int32))

    places = tile_row(match_blocks, chunks)
    own = places[0]
    prev = exchange(
        jnp.concatenate([places[1], match_class], axis=0), "sec", [(i, i + 1) for i in range(sections - 1)]
    )
    field, own_entry, own_stiff, own_stiff_line = call(
        "own",
        own_kernel,
        [SM, HBM, HBM, HBM],
        [big, send, (VM, f32(matches, LANES)), (VM, f32(1, matches))],
        scratch_shapes=[
            pltpu.SMEM(stiff_table.shape, jnp.float32),
            pltpu.VMEM(match_class.shape, jnp.int32),
            pltpu.SemaphoreType.DMA((3,)),
        ],
    )(own, stiff_table, match_class, tiled(displacement[:, 0]))
    entry, stiff, rows, stiff_line, send_x, send_z, halo_a, halo_b = call(
        "first",
        functools.partial(first_kernel, chunks),
        [SM, VM, VM, SM, VM, VM, VM, VM],
        [entries, (VM, f32(count, LANES)), rows_shape, (VM, f32(1, count)), send, send, halo, halo],
    )(prev, prev, own, stiff_table, field, own_entry, own_stiff, own_stiff_line)

    for sweep in range(ITERS):
        got_x = exchange(send_x, "sec", near)
        got_z = exchange(send_z, "sec", far)
        got_a = exchange(halo_a, "tile", near_tile)
        got_b = exchange(halo_b, "tile", far_tile)
        if sweep == 0:
            same, weight, factor = call(
                "setup",
                functools.partial(setup_kernel, chunks),
                [SM, VM, VM, HBM],
                [(VM, jax.ShapeDtypeStruct((total, count), jnp.bfloat16)), wide, wide],
                scratch_shapes=[
                    pltpu.VMEM((blocks, LANES), jnp.float32),
                    pltpu.VMEM((total, LANES), jnp.float32),
                    pltpu.VMEM((total, LANES), jnp.float32),
                    pltpu.SemaphoreType.DMA,
                ],
            )(rows, rows, stiff_line, tiled(spring[0]))
            (nearby,) = call("inner", functools.partial(inner_kernel, chunks), [VM], [big])(field)
        else:
            field, nearby = call(
                "inner",
                functools.partial(scatter_inner_kernel, chunks),
                [SM, VM, VM],
                [big, big],
                input_output_aliases={2: 0},
            )(rows, entry, nearby)
        nearby, base = call(
            "edge",
            functools.partial(edge_kernel, chunks),
            [SM] + [VM] * 9,
            [big, entries],
            input_output_aliases={9: 0},
        )(rows, field, entry, got_a, got_b, same, stiff, weight, factor, nearby)
        if sweep < ITERS - 1:
            entry, send_x, send_z, halo_a, halo_b = call(
                "step", functools.partial(step_kernel, chunks), [VM] * 6, [entries, send, send, halo, halo]
            )(got_x, got_z, base, same, factor, stiff)
    _, out = call(
        "last",
        last_kernel,
        [SM] + [VM] * 6,
        [big, (HBM, f32(fields, blocks, LANES))],
        scratch_shapes=[pltpu.VMEM((fields, total, LANES), jnp.float32), pltpu.SemaphoreType.DMA((2,))],
        input_output_aliases={1: 0},
    )(rows, nearby, got_x, got_z, base, same, factor)
    return untiled(out)[:, None]


def solution(mesh):
    placed = (
        P(None, "sec", "tile", None),
        P("sec", "tile", None),
        P(),
        P(None, "sec", "tile"),
        P("sec", "tile"),
    )
    return jax.shard_map(
        on_device,
        mesh=mesh,
        in_specs=placed,
        out_specs=P(None, "sec", "tile", None),
        check_vma=False,
    )
```

profile of v0, /device:TPU:3, one launch (start us, length us, event | category | flops | bytes accessed | tf_op | source)
XLA Modules:
  0.0 60.6 jit_solution(537503328414697843)
XLA Ops:
  0.0 0.7 %fusion = s32[2,1,256]{2,1,0:T(1,128)S(1)} fusion(s32[2,1,256]{2,1,0:T(1,128)} %param.8), kind=kLoop, calls=%fused_computation.10 | loop fusion | flops 21504 | bytes 4096 | tf_op jit(solution)/shard_map/add | solution.py:24
  0.7 0.7 %pad_add_fusion = s32[2,256]{1,0:T(2,128)S(1)} fusion(s32[1,256]{1,0:T(1,128)} %classes.1, s32[1,256]{1,0:T(1,128)S(1)} %get-tuple-element.78), kind=kLoop, calls=%fused_computation.13 | loop fusion | flops 512 | bytes 4096 | tf_op jit(solution)/shard_map/concatenate | solution.py:345
  1.4 3.2 %collective-permute-start = (s32[2,256]{1,0:T(2,128)S(1)}, s32[2,256]{1,0:T(2,128)S(1)}, u32[]{:S(2)}, u32[]{:S(2)}) collective-permute-start(s32[2,256]{1,0:T(2,128)S(1)} %pad_add_fusion), channel_id=1, source_target_pairs={{0,4},{4,8},{8,12},{12,16},{16,20},{20,24},{24,28},{1,5},{5,9},{9,... | collective-permute-start | bytes 6152 | tf_op jit(solution)/shard_map/ppermute | solution.py:293
  4.6 0.0 copy-start
  4.6 2.2 %copy-done = f32[2,1,256,2048]{3,2,1,0:T(8,128)S(1)} copy-done((f32[2,1,256,2048]{3,2,1,0:T(8,128)S(1)}, f32[2,1,256,2048]{3,2,1,0:T(8,128)}, u32[]{:S(2)}) %copy-start) | copy-done | bytes 4194328
  6.8 0.0 copy-start.2
  6.8 0.7 %copy-done.2 = s32[1,256]{1,0:T(1,128)S(1)} copy-done((s32[1,256]{1,0:T(1,128)S(1)}, s32[1,256]{1,0:T(1,128)}, u32[]{:S(2)}) %copy-start.2) | copy-done | bytes 1048
  7.5 0.0 copy-start.3
  7.5 0.7 %copy-done.3 = f32[8]{0:T(128)S(1)} copy-done((f32[8]{0:T(128)S(1)}, f32[8]{0:T(128)}, u32[]{:S(2)}) %copy-start.3) | copy-done | bytes 56
  8.1 1.9 %own.1 = (f32[2,4096,128]{2,1,0:T(8,128)S(1)}, f32[2,256,128]{2,1,0:T(8,128)S(1)}, f32[256,128]{1,0:T(8,128)S(1)}, f32[1,256]{1,0:T(1,128)S(1)}) custom-call(s32[1,256]{1,0:T(1,128)S(1)} %get-tuple-element.77.own.own_line, f32[8]{0:T(128)S(1)} %copy-done.3, s32[1,256]{1,0:T(1,128)S(1)} %copy-done.2, f32[2,4096,128]{2,1,0:T(8,128)S(1)} %bitcast.19), custom_call_target="tpu_custom_call" | custom-call | tf_op jit(solution)/shard_map/own/pallas_call | solution.py:347
  10.1 0.0 collective-permute-done.prev.prev_line
  10.1 1.4 %first.1 = (f32[2,544,128]{2,1,0:T(8,128)S(1)}, f32[512,128]{1,0:T(8,128)S(1)}, s32[1,512]{1,0:T(1,128)S(1)}, f32[1,512]{1,0:T(1,128)S(1)}, f32[2,256,128]{2,1,0...) custom-call(s32[2,256]{1,0:T(2,128)S(1)} %collective-permute-done.prev.prev_line, ...), custom_call_target="tpu_custom_call" | custom-call | tf_op jit(solution)/shard_map/first/pallas_call | solution.py:358
  11.5 0.3 collective-permute-start.1
  11.8 4.2 %collective-permute-start.2 = (f32[2,256,128]{2,1,0:T(8,128)S(1)}, f32[2,256,128]{2,1,0:T(8,128)S(1)}, u32[]{:S(2)}, u32[]{:S(2)}) collective-permute-start(f32[2,256,128]{2,1,0:T(8,128)S(1)} %get-tuple-element.47), channel_id=1, source_target_pairs={{4,8},{8,4},{12,16},{16,12},{20,24},{24,20},{5,9},{9,5},{13,17},{1... | collective-permute-start | bytes 786440 | tf_op jit(solution)/shard_map/ppermute | solution.py:293
  16.0 1.6 %collective-permute-start.3 = (f32[2,16,128]{2,1,0:T(8,128)S(1)}, f32[2,16,128]{2,1,0:T(8,128)S(1)}, u32[]{:S(2)}, u32[]{:S(2)}) collective-permute-start(f32[2,16,128]{2,1,0:T(8,128)S(1)} %get-tuple-element.49), channel_id=1, source_target_pairs={{0,1},{1,0},{2,3},{3,2},{4,5},{5,4},{6,7},{7,6},{8,9},{9,8},{10,11... | collective-permute-start | bytes 49160 | tf_op jit(solution)/shard_map/ppermute | solution.py:293
  17.5 0.0 copy-start.1
  17.5 3.2 %collective-permute-start.4 = (f32[2,16,128]{2,1,0:T(8,128)S(1)}, f32[2,16,128]{2,1,0:T(8,128)S(1)}, u32[]{:S(2)}, u32[]{:S(2)}) collective-permute-start(f32[2,16,128]{2,1,0:T(8,128)S(1)} %get-tuple-element.50), channel_id=1, source_target_pairs={{1,2},{2,1},{5,6},{6,5},{9,10},{10,9},{13,14},{14,13},{17,18},{18,... | collective-permute-start | bytes 49160 | tf_op jit(solution)/shard_map/ppermute | solution.py:293
  20.7 3.1 %inner.3.partial = f32[2,4096,128]{2,1,0:T(8,128)S(1)} custom-call(f32[2,4096,128]{2,1,0:T(8,128)S(1)} %get-tuple-element.41.field), custom_call_target="tpu_custom_call" | custom-call | tf_op jit(solution)/shard_map/inner/pallas_call | solution.py:383
  23.9 0.0 copy-done.1
  23.9 3.1 %setup.1 = (bf16[544,512]{1,0:T(8,128)(2,1)S(1)}, f32[544,128]{1,0:T(8,128)S(1)}, f32[544,128]{1,0:T(8,128)S(1)}) custom-call(s32[1,512]{1,0:T(1,128)S(1)} %get-tuple-element.45.rows.rows_line, s32[1,512]{1,0:T(1,128)S(1)} %get-tuple-element.45.rows.rows_line, f32[1,512]{1,0:T(1,128)S(1)} %get-tuple-element.51.stiff_line, f32[4096,128]{1,0:T(8,128)S(1)} %bitcast.20), custom_call_target="tpu_custom_call" | custom-call | tf_op jit(solution)/shard_map/setup/pallas_call | solution.py:371
  27.0 0.0 collective-permute-done.3.got_a
  27.0 0.0 collective-permute-done.4.got_b
  27.0 2.1 %edge.3 = (f32[2,4096,128]{2,1,0:T(8,128)S(1)}, f32[2,544,128]{2,1,0:T(8,128)S(1)}) custom-call(s32[1,512]{1,0:T(1,128)S(1)} %get-tuple-element.45.rows.rows_line, f32[2,4096,128]{2,1,0:T(8,128)S(1)} %get-tuple-element.41.field, f32[2,544,128]{2,1,0:T(8,128)S(1)} %get-tuple-element.48.entry, ...), custom_call_target="tpu_custom_call", output_to_operand_aliasing={{0}: (9, {})} | custom-call | tf_op jit(solution)/shard_map/edge/pallas_call | solution.py:392
  29.1 0.0 collective-permute-done.1.got_x
  29.2 0.0 collective-permute-done.2.got_z
  29.2 0.5 step.2
  29.7 0.1 collective-permute-start.5
  29.7 4.4 %collective-permute-start.6 = (f32[2,256,128]{2,1,0:T(8,128)S(1)}, f32[2,256,128]{2,1,0:T(8,128)S(1)}, u32[]{:S(2)}, u32[]{:S(2)}) collective-permute-start(f32[2,256,128]{2,1,0:T(8,128)S(1)} %get-tuple-element.58), channel_id=1, source_target_pairs={{4,8},{8,4},{12,16},{16,12},{20,24},{24,20},{5,9},{9,5},{13,17},{1... | collective-permute-start | bytes 786440 | tf_op jit(solution)/shard_map/ppermute | solution.py:293
  34.1 0.1 collective-permute-start.7
  34.2 3.1 %collective-permute-start.8 = (f32[2,16,128]{2,1,0:T(8,128)S(1)}, f32[2,16,128]{2,1,0:T(8,128)S(1)}, u32[]{:S(2)}, u32[]{:S(2)}) collective-permute-start(f32[2,16,128]{2,1,0:T(8,128)S(1)} %get-tuple-element.63), channel_id=1, source_target_pairs={{1,2},{2,1},{5,6},{6,5},{9,10},{10,9},{13,14},{14,13},{17,18},{18,... | collective-permute-start | bytes 49160 | tf_op jit(solution)/shard_map/ppermute | solution.py:293
  37.2 4.4 %inner.4 = (f32[2,4096,128]{2,1,0:T(8,128)S(1)}, f32[2,4096,128]{2,1,0:T(8,128)S(1)}) custom-call(s32[1,512]{1,0:T(1,128)S(1)} %get-tuple-element.45.rows.rows_line, f32[2,544,128]{2,1,0:T(8,128)S(1)} %get-tuple-element.59.entry, f32[2,4096,128]{2,1,0:T(8,128)S(1)} %get-tuple-element.60.stale), custom_call_target="tpu_custom_call", output_to_operand_aliasing={{0}: (2, {})} | custom-call | tf_op jit(solution)/shard_map/inner/pallas_call | solution.py:385
  41.6 0.0 collective-permute-done.7.got_a
  41.6 0.0 collective-permute-done.8.got_b
  41.6 2.1 %edge.4 = (f32[2,4096,128]{2,1,0:T(8,128)S(1)}, f32[2,544,128]{2,1,0:T(8,128)S(1)}) custom-call(s32[1,512]{1,0:T(1,128)S(1)} %get-tuple-element.45.rows.rows_line, f32[2,4096,128]{2,1,0:T(8,128)S(1)} %get-tuple-element.61.field, f32[2,544,128]{2,1,0:T(8,128)S(1)} %get-tuple-element.59.entry, ...), custom_call_target="tpu_custom_call", output_to_operand_aliasing={{0}: (9, {})} | custom-call | tf_op jit(solution)/shard_map/edge/pallas_call | solution.py:392
  43.7 0.0 collective-permute-done.5.got_x
  43.8 0.0 collective-permute-done.6.got_z
  43.8 0.5 step.3
  44.2 0.1 collective-permute-start.11
  44.3 2.8 %collective-permute-start.12 = (f32[2,256,128]{2,1,0:T(8,128)S(1)}, f32[2,256,128]{2,1,0:T(8,128)S(1)}, u32[]{:S(2)}, u32[]{:S(2)}) collective-permute-start(f32[2,256,128]{2,1,0:T(8,128)S(1)} %get-tuple-element.74), channel_id=1, source_target_pairs={{4,8},{8,4},{12,16},{16,12},{20,24},{24,20},{5,9},{9,5},{13,17},{1... | collective-permute-start | bytes 786440 | tf_op jit(solution)/shard_map/ppermute | solution.py:293
  47.2 0.1 collective-permute-start.9
  47.3 3.1 %collective-permute-start.10 = (f32[2,16,128]{2,1,0:T(8,128)S(1)}, f32[2,16,128]{2,1,0:T(8,128)S(1)}, u32[]{:S(2)}, u32[]{:S(2)}) collective-permute-start(f32[2,16,128]{2,1,0:T(8,128)S(1)} %get-tuple-element.70), channel_id=1, source_target_pairs={{1,2},{2,1},{5,6},{6,5},{9,10},{10,9},{13,14},{14,13},{17,18},{18,... | collective-permute-start | bytes 49160 | tf_op jit(solution)/shard_map/ppermute | solution.py:293
  50.3 4.4 %inner.5 = (f32[2,4096,128]{2,1,0:T(8,128)S(1)}, f32[2,4096,128]{2,1,0:T(8,128)S(1)}) custom-call(s32[1,512]{1,0:T(1,128)S(1)} %get-tuple-element.45.rows.rows_line, f32[2,544,128]{2,1,0:T(8,128)S(1)} %get-tuple-element.66.entry, f32[2,4096,128]{2,1,0:T(8,128)S(1)} %get-tuple-element.67.stale), custom_call_target="tpu_custom_call", output_to_operand_aliasing={{0}: (2, {})} | custom-call | tf_op jit(solution)/shard_map/inner/pallas_call | solution.py:385
  54.7 0.0 collective-permute-done.9.got_a
  54.7 0.0 collective-permute-done.10.got_b
  54.7 2.1 %edge.5 = (f32[2,4096,128]{2,1,0:T(8,128)S(1)}, f32[2,544,128]{2,1,0:T(8,128)S(1)}) custom-call(s32[1,512]{1,0:T(1,128)S(1)} %get-tuple-element.45.rows.rows_line, f32[2,4096,128]{2,1,0:T(8,128)S(1)} %get-tuple-element.68.field, f32[2,544,128]{2,1,0:T(8,128)S(1)} %get-tuple-element.66.entry, ...), custom_call_target="tpu_custom_call", output_to_operand_aliasing={{0}: (9, {})} | custom-call | tf_op jit(solution)/shard_map/edge/pallas_call | solution.py:392
  56.8 0.0 collective-permute-done.11.got_x
  56.8 0.0 collective-permute-done.12.got_z
  56.8 3.7 %last.1 = (f32[2,4096,128]{2,1,0:T(8,128)S(1)}, f32[2,4096,128]{2,1,0:T(8,128)}) custom-call(s32[1,512]{1,0:T(1,128)S(1)} %get-tuple-element.45.rows.rows_line, f32[2,4096,128]{2,1,0:T(8,128)S(1)} %get-tuple-element.72.stale, f32[2,256,128]{2,1,0:T(8,128)S(1)} %collective-permute-done.11.got_x, ...), custom_call_target="tpu_custom_call", output_to_operand_aliasing={{0}: (1, {})} | custom-call | tf_op jit(solution)/shard_map/last/pallas_call | solution.py:403
  (1 shorter events, 0.0 us)
Async XLA Ops:
  1.4 8.6 %collective-permute-start = (s32[2,256]{1,0:T(2,128)S(1)}, s32[2,256]{1,0:T(2,128)S(1)}, u32[]{:S(2)}, u32[]{:S(2)}) collective-permute-start(s32[2,256]{1,0:T(2,128)S(1)} %pad_add_fusion), channel_id=1, source_target_pairs={{0,4},{4,8},{8,12},{12,16},{16,20},{20,24},{24,28},{1,5},{5,9},{9,... | collective-permute-start | bytes 6152 | tf_op jit(solution)/shard_map/ppermute | solution.py:293
  4.6 2.2 %copy-start = (f32[2,1,256,2048]{3,2,1,0:T(8,128)S(1)}, f32[2,1,256,2048]{3,2,1,0:T(8,128)}, u32[]{:S(2)}) copy-start(f32[2,1,256,2048]{3,2,1,0:T(8,128)} %param.5) | copy-start | bytes 12582916
  6.8 0.7 %copy-start.2 = (s32[1,256]{1,0:T(1,128)S(1)}, s32[1,256]{1,0:T(1,128)}, u32[]{:S(2)}) copy-start(s32[1,256]{1,0:T(1,128)} %classes.1) | copy-start | bytes 3076
  7.5 0.7 %copy-start.3 = (f32[8]{0:T(128)S(1)}, f32[8]{0:T(128)}, u32[]{:S(2)}) copy-start(f32[8]{0:T(128)} %table.3) | copy-start | bytes 100
  11.5 17.6 %collective-permute-start.1 = (f32[2,256,128]{2,1,0:T(8,128)S(1)}, f32[2,256,128]{2,1,0:T(8,128)S(1)}, u32[]{:S(2)}, u32[]{:S(2)}) collective-permute-start(f32[2,256,128]{2,1,0:T(8,128)S(1)} %get-tuple-element.46), channel_id=1, source_target_pairs={{0,4},{4,0},{8,12},{12,8},{16,20},{20,16},{24,28},{28,24},{1,5},{5... | collective-permute-start | bytes 786440 | tf_op jit(solution)/shard_map/ppermute | solution.py:293
  11.8 17.4 %collective-permute-start.2 = (f32[2,256,128]{2,1,0:T(8,128)S(1)}, f32[2,256,128]{2,1,0:T(8,128)S(1)}, u32[]{:S(2)}, u32[]{:S(2)}) collective-permute-start(f32[2,256,128]{2,1,0:T(8,128)S(1)} %get-tuple-element.47), channel_id=1, source_target_pairs={{4,8},{8,4},{12,16},{16,12},{20,24},{24,20},{5,9},{9,5},{13,17},{1... | collective-permute-start | bytes 786440 | tf_op jit(solution)/shard_map/ppermute | solution.py:293
  16.0 11.1 %collective-permute-start.3 = (f32[2,16,128]{2,1,0:T(8,128)S(1)}, f32[2,16,128]{2,1,0:T(8,128)S(1)}, u32[]{:S(2)}, u32[]{:S(2)}) collective-permute-start(f32[2,16,128]{2,1,0:T(8,128)S(1)} %get-tuple-element.49), channel_id=1, source_target_pairs={{0,1},{1,0},{2,3},{3,2},{4,5},{5,4},{6,7},{7,6},{8,9},{9,8},{10,11... | collective-permute-start | bytes 49160 | tf_op jit(solution)/shard_map/ppermute | solution.py:293
  17.5 6.3 %copy-start.1 = (f32[1,256,2048]{2,1,0:T(8,128)S(1)}, f32[1,256,2048]{2,1,0:T(8,128)}, u32[]{:S(2)}) copy-start(f32[1,256,2048]{2,1,0:T(8,128)} %param.6) | copy-start | bytes 6291460
  17.5 9.5 %collective-permute-start.4 = (f32[2,16,128]{2,1,0:T(8,128)S(1)}, f32[2,16,128]{2,1,0:T(8,128)S(1)}, u32[]{:S(2)}, u32[]{:S(2)}) collective-permute-start(f32[2,16,128]{2,1,0:T(8,128)S(1)} %get-tuple-element.50), channel_id=1, source_target_pairs={{1,2},{2,1},{5,6},{6,5},{9,10},{10,9},{13,14},{14,13},{17,18},{18,... | collective-permute-start | bytes 49160 | tf_op jit(solution)/shard_map/ppermute | solution.py:293
  29.7 14.1 %collective-permute-start.5 = (f32[2,256,128]{2,1,0:T(8,128)S(1)}, f32[2,256,128]{2,1,0:T(8,128)S(1)}, u32[]{:S(2)}, u32[]{:S(2)}) collective-permute-start(f32[2,256,128]{2,1,0:T(8,128)S(1)} %get-tuple-element.57), channel_id=1, source_target_pairs={{0,4},{4,0},{8,12},{12,8},{16,20},{20,16},{24,28},{28,24},{1,5},{5... | collective-permute-start | bytes 786440 | tf_op jit(solution)/shard_map/ppermute | solution.py:293
  29.7 14.0 %collective-permute-start.6 = (f32[2,256,128]{2,1,0:T(8,128)S(1)}, f32[2,256,128]{2,1,0:T(8,128)S(1)}, u32[]{:S(2)}, u32[]{:S(2)}) collective-permute-start(f32[2,256,128]{2,1,0:T(8,128)S(1)} %get-tuple-element.58), channel_id=1, source_target_pairs={{4,8},{8,4},{12,16},{16,12},{20,24},{24,20},{5,9},{9,5},{13,17},{1... | collective-permute-start | bytes 786440 | tf_op jit(solution)/shard_map/ppermute | solution.py:293
  34.1 7.5 %collective-permute-start.7 = (f32[2,16,128]{2,1,0:T(8,128)S(1)}, f32[2,16,128]{2,1,0:T(8,128)S(1)}, u32[]{:S(2)}, u32[]{:S(2)}) collective-permute-start(f32[2,16,128]{2,1,0:T(8,128)S(1)} %get-tuple-element.62), channel_id=1, source_target_pairs={{0,1},{1,0},{2,3},{3,2},{4,5},{5,4},{6,7},{7,6},{8,9},{9,8},{10,11... | collective-permute-start | bytes 49160 | tf_op jit(solution)/shard_map/ppermute | solution.py:293
  34.2 7.4 %collective-permute-start.8 = (f32[2,16,128]{2,1,0:T(8,128)S(1)}, f32[2,16,128]{2,1,0:T(8,128)S(1)}, u32[]{:S(2)}, u32[]{:S(2)}) collective-permute-start(f32[2,16,128]{2,1,0:T(8,128)S(1)} %get-tuple-element.63), channel_id=1, source_target_pairs={{1,2},{2,1},{5,6},{6,5},{9,10},{10,9},{13,14},{14,13},{17,18},{18,... | collective-permute-start | bytes 49160 | tf_op jit(solution)/shard_map/ppermute | solution.py:293
  44.2 12.6 %collective-permute-start.11 = (f32[2,256,128]{2,1,0:T(8,128)S(1)}, f32[2,256,128]{2,1,0:T(8,128)S(1)}, u32[]{:S(2)}, u32[]{:S(2)}) collective-permute-start(f32[2,256,128]{2,1,0:T(8,128)S(1)} %get-tuple-element.73), channel_id=1, source_target_pairs={{0,4},{4,0},{8,12},{12,8},{16,20},{20,16},{24,28},{28,24},{1,5},{5... | collective-permute-start | bytes 786440 | tf_op jit(solution)/shard_map/ppermute | solution.py:293
  44.3 12.5 %collective-permute-start.12 = (f32[2,256,128]{2,1,0:T(8,128)S(1)}, f32[2,256,128]{2,1,0:T(8,128)S(1)}, u32[]{:S(2)}, u32[]{:S(2)}) collective-permute-start(f32[2,256,128]{2,1,0:T(8,128)S(1)} %get-tuple-element.74), channel_id=1, source_target_pairs={{4,8},{8,4},{12,16},{16,12},{20,24},{24,20},{5,9},{9,5},{13,17},{1... | collective-permute-start | bytes 786440 | tf_op jit(solution)/shard_map/ppermute | solution.py:293
  47.2 7.5 %collective-permute-start.9 = (f32[2,16,128]{2,1,0:T(8,128)S(1)}, f32[2,16,128]{2,1,0:T(8,128)S(1)}, u32[]{:S(2)}, u32[]{:S(2)}) collective-permute-start(f32[2,16,128]{2,1,0:T(8,128)S(1)} %get-tuple-element.69), channel_id=1, source_target_pairs={{0,1},{1,0},{2,3},{3,2},{4,5},{5,4},{6,7},{7,6},{8,9},{9,8},{10,11... | collective-permute-start | bytes 49160 | tf_op jit(solution)/shard_map/ppermute | solution.py:293
  47.3 7.5 %collective-permute-start.10 = (f32[2,16,128]{2,1,0:T(8,128)S(1)}, f32[2,16,128]{2,1,0:T(8,128)S(1)}, u32[]{:S(2)}, u32[]{:S(2)}) collective-permute-start(f32[2,16,128]{2,1,0:T(8,128)S(1)} %get-tuple-element.70), channel_id=1, source_target_pairs={{1,2},{2,1},{5,6},{6,5},{9,10},{10,9},{13,14},{14,13},{17,18},{18,... | collective-permute-start | bytes 49160 | tf_op jit(solution)/shard_map/ppermute | solution.py:293
where the time goes:
time: 60.9 us; the launch traced here: 60.6 us
  Pallas kernels  29.3 us (48%)
  starting transfers between devices  26 us (43%)
  local copies, waits for them, and re-layouts  3.52 us (6%)
  other arithmetic  1.41 us (2%)
    ppermute x13, starting transfers between devices, exchange(): return lax.ppermute(array, axis, pairs)  26 us
    pallas_call x2, Pallas kernels, on_device(): call('inner', functools.partial(scatter_inner_kernel, chunks), [SM, VM, V...  8.73 us
    pallas_call x3, Pallas kernels, on_device(): call('edge', functools.partial(edge_kernel, chunks), [SM] + [VM] * 9, [bi...  6.29 us
    pallas_call x1, Pallas kernels, on_device(): call('last', last_kernel, [SM] + [VM] * 6, [big, (HBM, f32(fields, blocks...  3.73 us
    unnamed x8, local copies, waits for them, and re-layouts  3.52 us
    pallas_call x1, Pallas kernels, on_device(): call('setup', functools.partial(setup_kernel, chunks), [SM, VM, VM, HBM],...  3.13 us
    pallas_call x1, Pallas kernels, on_device(): call('inner', functools.partial(inner_kernel, chunks), [VM], [big])(field)  3.12 us
    pallas_call x1, Pallas kernels, on_device(): call('own', own_kernel, [SM, HBM, HBM, HBM], [big, send, (VM, f32(matches...  1.93 us
  transfers between devices with their start and end apart: 13, of which 0 were waited for; matrix products, arithmetic and copies ran while one was open for 0% of the time, Pallas kernels for 38%

commit v1 on v0

v1 whole, which is shorter than its diff:
```python
import functools
import jax
import jax.numpy as jnp
from jax import lax
from jax.experimental import pallas as pl
from jax.experimental.pallas import tpu as pltpu
from jax.sharding import PartitionSpec as P

ITERS = 3
LOADS = 4
OWN_VMEM = 47
LANES = 128
SUB = 8

VM = pl.BlockSpec(memory_space=pltpu.VMEM)
SM = pl.BlockSpec(memory_space=pltpu.SMEM)
HBM = pl.BlockSpec(memory_space=pltpu.MemorySpace.HBM)


def f32(*shape):
    return jax.ShapeDtypeStruct(shape, jnp.float32)


def tile_row(block, chunks):
    row = block // chunks
    return (row // SUB) * (SUB * chunks) + (block % chunks) * SUB + row % SUB


def pieces(x):
    high = x.astype(jnp.bfloat16)
    low = (x - high.astype(jnp.float32)).astype(jnp.bfloat16)
    return high, low


def summed(same, x):
    high, low = pieces(x)
    return jnp.dot(same, high, preferred_element_type=jnp.float32) + jnp.dot(
        same, low, preferred_element_type=jnp.float32
    )


def parity(axis):
    return lax.axis_index(axis) % 2


def send_edges(entry, halo_a, halo_b, count, chunks):
    odd_tile = parity("tile")
    low = pl.multiple_of(count + (1 - odd_tile) * chunks, SUB)
    high = pl.multiple_of(count + odd_tile * chunks, SUB)
    halo_a[...] = entry[:, pl.ds(low, chunks), :]
    halo_b[...] = entry[:, pl.ds(high, chunks), :]


def columns(line):
    return jnp.concatenate(
        [
            jnp.broadcast_to(line[:, at : at + LANES], (LANES, LANES)).T
            for at in range(0, line.shape[1], LANES)
        ],
        axis=0,
    )


def each_slot(count, rows, body):
    def some(step, carry):
        for inner in range(8):
            slot = step * 8 + inner
            body(slot, rows(slot))
        return carry

    lax.fori_loop(0, count // 8, some, 0)


def into_smem(line, staged, scalars, sem):
    staged[...] = line.astype(jnp.int32)
    copy = pltpu.make_async_copy(staged, scalars, sem)
    copy.start()
    return copy


def load_parts(source, target, sem, pieces_each):
    rows = source.shape[1] // pieces_each
    copies = []
    for part in range(source.shape[0]):
        for piece in range(pieces_each):
            at = pl.ds(piece * rows, rows)
            copies.append(
                pltpu.make_async_copy(
                    source.at[part, at, :], target.at[part, at, :], sem.at[part * pieces_each + piece]
                )
            )
    return copies


def own_kernel(packed, displacement, field, entry, stiff, line, staged, scalars, sem, load_sem):
    loads = load_parts(displacement, field, load_sem, LOADS)
    for copy in loads:
        copy.start()
    listed = into_smem(packed[0:1, :], staged, scalars, sem)
    alive = lax.axis_index("sec") < lax.axis_size("sec") - 1
    line[...] = packed[2:3, :] * alive.astype(jnp.float32)
    stiff[...] = columns(line[...])
    listed.wait()
    for copy in loads:
        copy.wait()

    def take(slot, row):
        for part in range(2):
            entry[part, pl.ds(slot, 1), :] = field[part, pl.ds(row, 1), :]

    each_slot(packed.shape[1], lambda j: scalars[0, j], take)


def first_kernel(chunks, packed, prev, field, own_entry, own_stiff, own_stiff_line, entry, stiff, rows, stiff_line, send_x, send_z, halo_a, halo_b, staged, scalars, taken, sem):
    blocks = field.shape[1]
    matches = own_entry.shape[1]
    count = 2 * matches
    listed = into_smem(prev[1:2, :], staged, scalars, sem)
    even = parity("sec") == 0
    line = prev[2:3, :] * (lax.axis_index("sec") > 0).astype(jnp.float32)
    stiff_prev = columns(line)
    own_rows, prev_rows = packed[0:1, :].astype(jnp.int32), prev[1:2, :].astype(jnp.int32)
    for out, first, second in ((rows, own_rows, prev_rows), (stiff_line, own_stiff_line[...], line)):
        out[:, :matches] = jnp.where(even, first, second)
        out[:, matches:] = jnp.where(even, second, first)
    for part in range(2):
        for chunk in range(chunks):
            entry[part, pl.ds(count + chunk, 1), :] = field[part, pl.ds(chunk * SUB, 1), :]
            entry[part, pl.ds(count + chunks + chunk, 1), :] = field[
                part, pl.ds(blocks - SUB * chunks + chunk * SUB + SUB - 1, 1), :
            ]
    send_edges(entry, halo_a, halo_b, count, chunks)
    listed.wait()

    def take(slot, row):
        for part in range(2):
            taken[part, pl.ds(slot, 1), :] = field[part, pl.ds(row, 1), :]

    each_slot(matches, lambda j: scalars[0, j], take)

    def place(values, coupling, at, send):
        stiff[at : at + matches, :] = coupling
        for part in range(2):
            value = values[part]
            entry[part, at : at + matches, :] = value
            send[part] = value * coupling

    @pl.when(even)
    def _():
        place(own_entry, own_stiff[...], 0, send_x)
        place(taken, stiff_prev, matches, send_z)

    @pl.when(jnp.logical_not(even))
    def _():
        place(taken, stiff_prev, 0, send_x)
        place(own_entry, own_stiff[...], matches, send_z)


def setup_kernel(chunks, rows, rows_line, stiff_line, spring, same, weight, factor, picked, column):
    blocks = spring.shape[0]
    count = rows_line.shape[1]
    total = count + 2 * chunks
    last = blocks - SUB * chunks + SUB - 1
    column[:count, :] = columns(rows_line[...].astype(jnp.float32))
    edge = lax.broadcasted_iota(jnp.int32, (chunks, LANES), 0) * SUB
    column[count : count + chunks, :] = edge.astype(jnp.float32)
    column[count + chunks :, :] = (edge + last).astype(jnp.float32)
    place = lax.broadcasted_iota(jnp.int32, (1, LANES), 1)
    edge_line = jnp.where(place < chunks, place * SUB, (place - chunks) * SUB + last)
    edge_line = jnp.where(place < 2 * chunks, edge_line, -1).astype(jnp.float32)

    def band(step, carry):
        at = pl.ds(pl.multiple_of(step * 32, 32), 32)
        col = column[at, :]
        total_stiff = jnp.zeros((32, LANES), jnp.float32)
        for piece in range(count // LANES):
            cut = slice(piece * LANES, (piece + 1) * LANES)
            equal = col == rows_line[:, cut].astype(jnp.float32)
            same[at, cut] = equal.astype(jnp.float32).astype(jnp.bfloat16)
            total_stiff += jnp.where(equal, stiff_line[:, cut], 0.0)
        same[at, count:] = (col == edge_line).astype(jnp.float32).astype(jnp.bfloat16)
        factor[at, :] = jnp.broadcast_to(jnp.sum(total_stiff, axis=1, keepdims=True), (32, LANES))
        return carry

    lax.fori_loop(0, total // 32, band, 0)

    def take(slot, row):
        picked[pl.ds(slot, 1), :] = spring[pl.ds(row, 1), :]

    each_slot(count, lambda j: rows[0, j], take)
    for chunk in range(chunks):
        take(count + chunk, chunk * SUB)
        take(count + chunks + chunk, chunk * SUB + last)
    spring_here = picked[...]
    inverse = 1.0 / (4.0 * spring_here + factor[...])
    weight[...] = 4.0 * spring_here * inverse
    factor[...] = 0.8 * inverse


def stencil(field, nearby, start, chunks, top=False, bottom=False):
    span = SUB * chunks
    lane = lax.broadcasted_iota(jnp.int32, (SUB, LANES), 1)
    sub = lax.broadcasted_iota(jnp.int32, (SUB, LANES), 0)
    for part in range(2):

        def at(offset):
            return field[part, pl.ds(start + offset, SUB), :]

        before = jnp.zeros((SUB, LANES), jnp.float32)
        here = at(0)
        for chunk in range(chunks):
            offset = chunk * SUB
            after = at(offset + SUB) if chunk < chunks - 1 else jnp.zeros((SUB, LANES), jnp.float32)
            if top:
                up = jnp.where(sub == 0, 0.0, pltpu.roll(here, 1, 0))
            else:
                up = jnp.where(sub == 0, at(offset - span + SUB - 1), at(offset - 1))
            if bottom:
                down = jnp.where(sub == SUB - 1, 0.0, pltpu.roll(here, SUB - 1, 0))
            else:
                down = jnp.where(sub == SUB - 1, at(offset + span - SUB + 1), at(offset + 1))
            left = pltpu.roll(jnp.where(lane == LANES - 1, before, here), 1, 1)
            right = pltpu.roll(jnp.where(lane == 0, after, here), LANES - 1, 1)
            nearby[part, pl.ds(start + offset, SUB), :] = 0.2 * (((up + down) + (left + right)) + here)
            before, here = here, after


def bulk(chunks, rows, field, entry, same, stiff, weight, factor, nearby, base):
    blocks = field.shape[1]
    span = SUB * chunks
    strips = blocks // span
    count = rows.shape[1]
    stencil(field, nearby, 0, chunks, top=True)
    stencil(field, nearby, blocks - span, chunks, bottom=True)

    def pair(step, carry):
        for inner in range(2):
            stencil(field, nearby, pl.multiple_of((1 + step * 2 + inner) * span, SUB), chunks)
        return carry

    lax.fori_loop(0, (strips - 2) // 2, pair, 0)

    def take(slot, row):
        for part in range(2):
            base[part, pl.ds(slot, 1), :] = nearby[part, pl.ds(row, 1), :]

    each_slot(count, lambda j: rows[0, j], take)
    for chunk in range(chunks):
        take(count + chunk, chunk * SUB)
        take(count + chunks + chunk, blocks - span + chunk * SUB + SUB - 1)
    own = jnp.concatenate([entry[part, :count, :] * stiff[...] for part in range(2)], axis=1)
    total = summed(same[:, :count], own)
    for part in range(2):
        value = entry[part]
        base[part] = (
            value
            + weight[...] * (base[part] - value)
            - factor[...] * total[:, part * LANES : (part + 1) * LANES]
        )


def halo_rows(got_a, got_b):
    odd_tile = parity("tile") == 1
    return [
        (
            0.2 * jnp.where(odd_tile, got_a[part], got_b[part]),
            0.2 * jnp.where(odd_tile, got_b[part], got_a[part]),
        )
        for part in range(2)
    ]


def add_halo(field, halos, chunks):
    last = field.shape[1] - SUB * chunks + SUB - 1
    for part, (above, below) in enumerate(halos):
        for chunk in range(chunks):
            for start, halo in ((0, above), (last, below)):
                at = pl.ds(start + chunk * SUB, 1)
                field[part, at, :] = field[part, at, :] + halo[chunk : chunk + 1, :]


def inner_kernel(chunks, rows, entry, same, stiff, weight, factor, field, nearby, base):
    bulk(chunks, rows, field, entry, same, stiff, weight, factor, nearby, base)


def scatter_inner_kernel(chunks, rows, entry, same, stiff, weight, factor, got_a, got_b, stale, field, nearby, base):
    add_halo(field, halo_rows(got_a, got_b), chunks)

    def put(slot, row):
        for part in range(2):
            field[part, pl.ds(row, 1), :] = entry[part, pl.ds(slot, 1), :]

    each_slot(rows.shape[1], lambda j: rows[0, j], put)
    bulk(chunks, rows, field, entry, same, stiff, weight, factor, nearby, base)


def new_entries(got_x, got_z, halos, base, same, weight, factor):
    count = 2 * got_x.shape[1]
    got = jnp.concatenate(
        [jnp.concatenate([got_x[part], got_z[part]], axis=0) for part in range(2)], axis=1
    )
    unused = same.shape[1] - count - 2 * halos[0][0].shape[0]
    edges = jnp.concatenate(
        [
            jnp.concatenate([above, below, jnp.zeros((unused, LANES), jnp.float32)], axis=0)
            for above, below in halos
        ],
        axis=1,
    )
    total = summed(same[:, :count], got)
    outside = summed(same[:, count:], edges)
    out = []
    for part in range(2):
        cut = slice(part * LANES, (part + 1) * LANES)
        out.append(base[part] + weight[...] * outside[:, cut] + factor[...] * total[:, cut])
    return out


def step_kernel(chunks, got_x, got_z, got_a, got_b, base, same, weight, factor, stiff, entry, send_x, send_z, halo_a, halo_b):
    matches = got_x.shape[1]
    count = 2 * matches
    halos = halo_rows(got_a, got_b)
    for part, value in enumerate(new_entries(got_x, got_z, halos, base, same, weight, factor)):
        entry[part] = value
        send_x[part] = value[:matches] * stiff[:matches, :]
        send_z[part] = value[matches:count] * stiff[matches:, :]
    send_edges(entry, halo_a, halo_b, count, chunks)


def last_kernel(chunks, rows, stale, got_x, got_z, got_a, got_b, base, same, weight, factor, nearby, out, entry, sem):
    halos = halo_rows(got_a, got_b)
    add_halo(nearby, halos, chunks)
    for part, value in enumerate(new_entries(got_x, got_z, halos, base, same, weight, factor)):
        entry[part] = value
    stores = load_parts(nearby, out, sem, LOADS)
    for part in range(2):

        def put(slot, row):
            nearby[part, pl.ds(row, 1), :] = entry[part, pl.ds(slot, 1), :]

        each_slot(rows.shape[1], lambda j: rows[0, j], put)
        for copy in stores[part * LOADS : (part + 1) * LOADS]:
            copy.start()
    for copy in stores:
        copy.wait()


def exchange(array, axis, pairs):
    return lax.ppermute(array, axis, pairs)


def pairs_from(first, size):
    out = []
    for i in range(first, size - 1, 2):
        out += [(i, i + 1), (i + 1, i)]
    return out


def on_device(displacement, spring, stiff_table, match_blocks, match_class):
    fields, single, height, breadth = displacement.shape
    chunks = breadth // LANES
    blocks = height * chunks
    matches = match_blocks.shape[2]
    count = 2 * matches
    total = count + 2 * chunks
    sections, tiles = lax.axis_size("sec"), lax.axis_size("tile")
    near, far = pairs_from(0, sections), pairs_from(1, sections)
    near_tile, far_tile = pairs_from(0, tiles), pairs_from(1, tiles)

    def tiled(x):
        lead = x.shape[:-2]
        x = x.reshape(lead + (height // SUB, SUB, chunks, LANES))
        return jnp.swapaxes(x, -3, -2).reshape(lead + (blocks, LANES))

    def untiled(x):
        lead = x.shape[:-2]
        x = x.reshape(lead + (height // SUB, chunks, SUB, LANES))
        return jnp.swapaxes(x, -3, -2).reshape(lead + (height, breadth))

    def call(name, kernel, ins, outs, vmem=24 << 20, **more):
        return pl.pallas_call(
            kernel,
            in_specs=ins,
            out_specs=tuple(spec for spec, _ in outs),
            out_shape=tuple(shape for _, shape in outs),
            compiler_params=pltpu.CompilerParams(vmem_limit_bytes=vmem),
            name=name,
            **more,
        )

    halo = (VM, f32(fields, chunks, LANES))
    send = (VM, f32(fields, matches, LANES))
    entries = (VM, f32(fields, total, LANES))
    big = (VM, f32(fields, blocks, LANES))
    wide = (VM, f32(total, LANES))
    rows_shape = (VM, jax.ShapeDtypeStruct((1, count), jnp.int32))

    level = jnp.arange(stiff_table.shape[0], dtype=jnp.int32)[:, None]
    coupling = jnp.sum(jnp.where(match_class == level, stiff_table[:, None], 0.0), axis=0, keepdims=True)
    places = tile_row(match_blocks[:, 0], chunks).astype(jnp.float32)
    packed = jnp.concatenate([places, coupling], axis=0)
    prev = exchange(packed, "sec", [(i, i + 1) for i in range(sections - 1)])
    staging = [
        pltpu.VMEM((1, matches), jnp.int32),
        pltpu.SMEM((1, matches), jnp.int32),
    ]
    field, own_entry, own_stiff, own_stiff_line = call(
        "own",
        own_kernel,
        [VM, HBM],
        [big, send, (VM, f32(matches, LANES)), (VM, f32(1, matches))],
        scratch_shapes=staging + [pltpu.SemaphoreType.DMA, pltpu.SemaphoreType.DMA((2 * LOADS,))],
        vmem=OWN_VMEM << 20,
    )(packed, tiled(displacement[:, 0]))
    entry, stiff, rows, stiff_line, send_x, send_z, halo_a, halo_b = call(
        "first",
        functools.partial(first_kernel, chunks),
        [VM] * 6,
        [entries, (VM, f32(count, LANES)), rows_shape, (VM, f32(1, count)), send, send, halo, halo],
        scratch_shapes=staging
        + [pltpu.VMEM((fields, matches, LANES), jnp.float32), pltpu.SemaphoreType.DMA],
    )(packed, prev, field, own_entry, own_stiff, own_stiff_line)

    for sweep in range(ITERS):
        if sweep > 0:
            past = (got_a, got_b)
        got_x = exchange(send_x, "sec", near)
        got_z = exchange(send_z, "sec", far)
        got_a = exchange(halo_a, "tile", near_tile)
        got_b = exchange(halo_b, "tile", far_tile)
        if sweep == 0:
            same, weight, factor = call(
                "setup",
                functools.partial(setup_kernel, chunks),
                [SM, VM, VM, VM],
                [(VM, jax.ShapeDtypeStruct((total, count + LANES), jnp.bfloat16)), wide, wide],
                scratch_shapes=[pltpu.VMEM((total, LANES), jnp.float32)] * 2,
            )(rows, rows, stiff_line, tiled(spring[0]))
            nearby, base = call(
                "inner", functools.partial(inner_kernel, chunks), [SM] + [VM] * 6, [big, entries]
            )(rows, entry, same, stiff, weight, factor, field)
        else:
            field, nearby, base = call(
                "inner",
                functools.partial(scatter_inner_kernel, chunks),
                [SM] + [VM] * 8,
                [big, big, entries],
                input_output_aliases={8: 0},
            )(rows, entry, same, stiff, weight, factor, *past, nearby)
        if sweep < ITERS - 1:
            entry, send_x, send_z, halo_a, halo_b = call(
                "step", functools.partial(step_kernel, chunks), [VM] * 9, [entries, send, send, halo, halo]
            )(got_x, got_z, got_a, got_b, base, same, weight, factor, stiff)
    _, out = call(
        "last",
        functools.partial(last_kernel, chunks),
        [SM] + [VM] * 9,
        [big, (HBM, f32(fields, blocks, LANES))],
        scratch_shapes=[
            pltpu.VMEM((fields, total, LANES), jnp.float32),
            pltpu.SemaphoreType.DMA((2 * LOADS,)),
        ],
        input_output_aliases={1: 0},
    )(rows, nearby, got_x, got_z, got_a, got_b, base, same, weight, factor)
    return untiled(out)[:, None]


def solution(mesh):
    placed = (
        P(None, "sec", "tile", None),
        P("sec", "tile", None),
        P(),
        P(None, "sec", "tile"),
        P("sec", "tile"),
    )
    return jax.shard_map(
        on_device,
        mesh=mesh,
        in_specs=placed,
        out_specs=P(None, "sec", "tile", None),
        check_vma=False,
    )
```

time: 60.9 us -> 57.8 us (0.949)
  local copies, waits for them, and re-layouts: 3.52 us -> 0.01 us
    unnamed x8 -> x2, local copies, waits for them, and re-layouts: 3.52 us -> 0.01 us
    reduce_sum x0 -> x1, other arithmetic: none -> 0.78 us  [on_device(): jnp.sum(jnp.where(match_class == level, stiff_table[:, None], 0.0), axis=...]
    add x1 -> x0, other arithmetic: 0.72 us -> none  [tile_row(): return row // SUB * (SUB * chunks) + block % chunks * SUB + row % SUB]
    convert_element_type x0 -> x1, other arithmetic: none -> 0.7 us  [on_device(): places = tile_row(match_blocks[:, 0], chunks).astype(jnp.float32)]
    concatenate x1, other arithmetic: 0.69 us -> 0.01 us  [on_device(): packed = jnp.concatenate([places, coupling], axis=0)]
    ppermute x13, starting transfers between devices: 26 us -> 26.6 us  [exchange(): return lax.ppermute(array, axis, pairs)]
    pallas_call x12 -> x9, Pallas kernels: 29.3 us -> 29.1 us  [the longest x2 11.8 us: on_device(): call('inner', functools.partial(scatter_inner_kernel, chunks), [SM] + [VM...]
  transfers between devices with their start and end apart: 13 -> 13, of which waited for: 0 -> 0; matrix products, arithmetic and copies ran while one was open for 0% -> 0% of each run, Pallas kernels for 38% -> 40%
where the time goes in v1:
time: 57.8 us; the launch traced here: 57.5 us
  Pallas kernels  29.1 us (50%)
  starting transfers between devices  26.6 us (46%)
  other arithmetic  1.49 us (3%)
    ppermute x13, starting transfers between devices, exchange(): return lax.ppermute(array, axis, pairs)  26.6 us
    pallas_call x2, Pallas kernels, on_device(): call('inner', functools.partial(scatter_inner_kernel, chunks), [SM] + [VM...  11.8 us
    pallas_call x1, Pallas kernels, on_device(): call('inner', functools.partial(inner_kernel, chunks), [SM] + [VM] * 6, [...  5.18 us
    pallas_call x1, Pallas kernels, on_device(): call('last', functools.partial(last_kernel, chunks), [SM] + [VM] * 9, [bi...  3.95 us
    pallas_call x1, Pallas kernels, on_device(): call('setup', functools.partial(setup_kernel, chunks), [SM, VM, VM, VM],...  3 us
    pallas_call x1, Pallas kernels, on_device(): call('own', own_kernel, [VM, HBM], [big, send, (VM, f32(matches, LANES)),...  2.78 us
    pallas_call x2, Pallas kernels, on_device(): call('step', functools.partial(step_kernel, chunks), [VM] * 9, [entries,...  1.33 us
  transfers between devices with their start and end apart: 13, of which 0 were waited for; matrix products, arithmetic and copies ran while one was open for 0% of the time, Pallas kernels for 40%

profile of v1, /device:TPU:3, one launch (start us, length us, event | category | flops | bytes accessed | tf_op | source)
XLA Modules:
  0.0 57.5 jit_solution(3729409606881735439)
XLA Ops:
  0.0 0.7 %fusion.3 = f32[2,256]{1,0:T(2,128)S(1)} fusion(s32[2,1,256]{2,1,0:T(1,128)} %param.8), kind=kLoop, calls=%fused_computation.18 | loop fusion | flops 22016 | bytes 4096 | tf_op jit(solution)/shard_map/convert_element_type | solution.py:400
  0.7 0.8 %select_reduce_fusion = f32[256]{0:T(256)S(1)} fusion(f32[8]{0:T(128)} %param.7, s32[256]{0:T(256)} %bitcast.36), kind=kLoop, calls=%fused_computation | loop fusion | flops 5888 | bytes 2080 | tf_op jit(solution)/shard_map/reduce_sum | solution.py:399
  1.5 3.2 %collective-permute-start = (f32[3,256]{1,0:T(4,128)S(1)}, f32[3,256]{1,0:T(4,128)S(1)}, u32[]{:S(2)}, u32[]{:S(2)}) collective-permute-start(f32[3,256]{1,0:T(4,128)S(1)} %pad_maximum_fusion.packed), channel_id=1, source_target_pairs={{0,4},{4,8},{8,12},{12,16},{16,20},{20,24},{24,28},{1,5},{5,9},{9,... | collective-permute-start | bytes 9224 | tf_op jit(solution)/shard_map/ppermute | solution.py:349
  4.7 0.0 copy-start
  4.7 2.8 %own.1 = (f32[2,4096,128]{2,1,0:T(8,128)S(1)}, f32[2,256,128]{2,1,0:T(8,128)S(1)}, f32[256,128]{1,0:T(8,128)S(1)}, f32[1,256]{1,0:T(1,128)S(1)}) custom-call(f32[3,256]{1,0:T(4,128)S(1)} %pad_maximum_fusion.packed, f32[2,4096,128]{2,1,0:T(8,128)} %bitcast.34), custom_call_target="tpu_custom_call" | custom-call | tf_op jit(solution)/shard_map/own/pallas_call | solution.py:407
  7.5 0.0 collective-permute-done.prev
  7.5 1.1 %first.1 = (f32[2,544,128]{2,1,0:T(8,128)S(1)}, f32[512,128]{1,0:T(8,128)S(1)}, s32[1,512]{1,0:T(1,128)S(1)}, f32[1,512]{1,0:T(1,128)S(1)}, f32[2,256,128]{2,1,0...) custom-call(f32[3,256]{1,0:T(4,128)S(1)} %pad_maximum_fusion.packed, ...), custom_call_target="tpu_custom_call" | custom-call | tf_op jit(solution)/shard_map/first/pallas_call | solution.py:415
  8.6 0.3 collective-permute-start.1
  8.9 4.2 %collective-permute-start.2 = (f32[2,256,128]{2,1,0:T(8,128)S(1)}, f32[2,256,128]{2,1,0:T(8,128)S(1)}, u32[]{:S(2)}, u32[]{:S(2)}) collective-permute-start(f32[2,256,128]{2,1,0:T(8,128)S(1)} %get-tuple-element.43), channel_id=1, source_target_pairs={{4,8},{8,4},{12,16},{16,12},{20,24},{24,20},{5,9},{9,5},{13,17},{1... | collective-permute-start | bytes 786440 | tf_op jit(solution)/shard_map/ppermute | solution.py:349
  13.1 1.6 %collective-permute-start.3 = (f32[2,16,128]{2,1,0:T(8,128)S(1)}, f32[2,16,128]{2,1,0:T(8,128)S(1)}, u32[]{:S(2)}, u32[]{:S(2)}) collective-permute-start(f32[2,16,128]{2,1,0:T(8,128)S(1)} %get-tuple-element.44), channel_id=1, source_target_pairs={{0,1},{1,0},{2,3},{3,2},{4,5},{5,4},{6,7},{7,6},{8,9},{9,8},{10,11... | collective-permute-start | bytes 49160 | tf_op jit(solution)/shard_map/ppermute | solution.py:349
  14.6 3.0 %collective-permute-start.4 = (f32[2,16,128]{2,1,0:T(8,128)S(1)}, f32[2,16,128]{2,1,0:T(8,128)S(1)}, u32[]{:S(2)}, u32[]{:S(2)}) collective-permute-start(f32[2,16,128]{2,1,0:T(8,128)S(1)} %get-tuple-element.45), channel_id=1, source_target_pairs={{1,2},{2,1},{5,6},{6,5},{9,10},{10,9},{13,14},{14,13},{17,18},{18,... | collective-permute-start | bytes 49160 | tf_op jit(solution)/shard_map/ppermute | solution.py:349
  17.7 0.0 copy-done
  17.7 3.0 %setup.1 = (bf16[544,640]{1,0:T(8,128)(2,1)S(1)}, f32[544,128]{1,0:T(8,128)S(1)}, f32[544,128]{1,0:T(8,128)S(1)}) custom-call(s32[1,512]{1,0:T(1,128)S(1)} %get-tuple-element.41.rows.rows_line, s32[1,512]{1,0:T(1,128)S(1)} %get-tuple-element.41.rows.rows_line, f32[1,512]{1,0:T(1,128)S(1)} %get-tuple-element.47.stiff_line, f32[4096,128]{1,0:T(8,128)S(1)} %bitcast.33), custom_call_target="tpu_custom_call" | custom-call | tf_op jit(solution)/shard_map/setup/pallas_call | solution.py:432
  20.7 5.2 %inner.3 = (f32[2,4096,128]{2,1,0:T(8,128)S(1)}, f32[2,544,128]{2,1,0:T(8,128)S(1)}) custom-call(s32[1,512]{1,0:T(1,128)S(1)} %get-tuple-element.41.rows.rows_line, f32[2,544,128]{2,1,0:T(8,128)S(1)} %get-tuple-element.46.entry, bf16[544,640]{1,0:T(8,128)(2,1)S(1)} %get-tuple-element.48.same, f32[512,128]{1,0:T(8,128)S(1)} %get-tuple-element.49.stiff, ...), custom_call_target="tpu_custom_call" | custom-call | tf_op jit(solution)/shard_map/inner/pallas_call | solution.py:439
  25.9 0.0 collective-permute-done.3.got_a
  25.9 0.0 collective-permute-done.4.got_b
  25.9 0.0 collective-permute-done.1.got_x
  25.9 0.0 collective-permute-done.2.got_z
  25.9 0.7 %step.2 = (f32[2,544,128]{2,1,0:T(8,128)S(1)}, f32[2,256,128]{2,1,0:T(8,128)S(1)}, f32[2,256,128]{2,1,0:T(8,128)S(1)}, f32[2,16,128]{2,1,0:T(8,128)S(1)}, f32[2,16,128]{2,1,0:T(8,128)S(1)}) custom-call(f32[2,256,128]{2,1,0:T(8,128)S(1)} %collective-permute-done.1.got_x, f32[2,256,128]{2,1,0:T(8,128)S(1)} %collective-permute-done.2.got_z, ...), custom_call_target="tpu_custom_call" | custom-call | tf_op jit(solution)/shard_map/step/pallas_call | solution.py:451
  26.6 0.1 collective-permute-start.5
  26.7 4.4 %collective-permute-start.6 = (f32[2,256,128]{2,1,0:T(8,128)S(1)}, f32[2,256,128]{2,1,0:T(8,128)S(1)}, u32[]{:S(2)}, u32[]{:S(2)}) collective-permute-start(f32[2,256,128]{2,1,0:T(8,128)S(1)} %get-tuple-element.54), channel_id=1, source_target_pairs={{4,8},{8,4},{12,16},{16,12},{20,24},{24,20},{5,9},{9,5},{13,17},{1... | collective-permute-start | bytes 786440 | tf_op jit(solution)/shard_map/ppermute | solution.py:349
  31.1 0.1 collective-permute-start.7
  31.1 3.1 %collective-permute-start.8 = (f32[2,16,128]{2,1,0:T(8,128)S(1)}, f32[2,16,128]{2,1,0:T(8,128)S(1)}, u32[]{:S(2)}, u32[]{:S(2)}) collective-permute-start(f32[2,16,128]{2,1,0:T(8,128)S(1)} %get-tuple-element.56), channel_id=1, source_target_pairs={{1,2},{2,1},{5,6},{6,5},{9,10},{10,9},{13,14},{14,13},{17,18},{18,... | collective-permute-start | bytes 49160 | tf_op jit(solution)/shard_map/ppermute | solution.py:349
  34.2 5.9 %inner.4 = (f32[2,4096,128]{2,1,0:T(8,128)S(1)}, f32[2,4096,128]{2,1,0:T(8,128)S(1)}, f32[2,544,128]{2,1,0:T(8,128)S(1)}) custom-call(s32[1,512]{1,0:T(1,128)S(1)} %get-tuple-element.41.rows.rows_line, f32[2,544,128]{2,1,0:T(8,128)S(1)} %get-tuple-element.57.entry, bf16[544,640]{1,0:T(8,128)(2,1)S(1)} %get-tuple-element.48.same, ...), custom_call_target="tpu_custom_call", output_to_operand_aliasing={{0}: (8, {})} | custom-call | tf_op jit(solution)/shard_map/inner/pallas_call | solution.py:443
  40.1 0.0 collective-permute-done.7.got_a
  40.1 0.0 collective-permute-done.8.got_b
  40.1 0.0 collective-permute-done.5.got_x
  40.2 0.0 collective-permute-done.6.got_z
  40.2 0.7 %step.3 = (f32[2,544,128]{2,1,0:T(8,128)S(1)}, f32[2,256,128]{2,1,0:T(8,128)S(1)}, f32[2,256,128]{2,1,0:T(8,128)S(1)}, f32[2,16,128]{2,1,0:T(8,128)S(1)}, f32[2,16,128]{2,1,0:T(8,128)S(1)}) custom-call(f32[2,256,128]{2,1,0:T(8,128)S(1)} %collective-permute-done.5.got_x, f32[2,256,128]{2,1,0:T(8,128)S(1)} %collective-permute-done.6.got_z, ...), custom_call_target="tpu_custom_call" | custom-call | tf_op jit(solution)/shard_map/step/pallas_call | solution.py:451
  40.8 0.1 collective-permute-start.9
  40.9 3.6 %collective-permute-start.10 = (f32[2,256,128]{2,1,0:T(8,128)S(1)}, f32[2,256,128]{2,1,0:T(8,128)S(1)}, u32[]{:S(2)}, u32[]{:S(2)}) collective-permute-start(f32[2,256,128]{2,1,0:T(8,128)S(1)} %get-tuple-element.64), channel_id=1, source_target_pairs={{4,8},{8,4},{12,16},{16,12},{20,24},{24,20},{5,9},{9,5},{13,17},{1... | collective-permute-start | bytes 786440 | tf_op jit(solution)/shard_map/ppermute | solution.py:349
  44.5 0.1 collective-permute-start.11
  44.6 3.1 %collective-permute-start.12 = (f32[2,16,128]{2,1,0:T(8,128)S(1)}, f32[2,16,128]{2,1,0:T(8,128)S(1)}, u32[]{:S(2)}, u32[]{:S(2)}) collective-permute-start(f32[2,16,128]{2,1,0:T(8,128)S(1)} %get-tuple-element.66), channel_id=1, source_target_pairs={{1,2},{2,1},{5,6},{6,5},{9,10},{10,9},{13,14},{14,13},{17,18},{18,... | collective-permute-start | bytes 49160 | tf_op jit(solution)/shard_map/ppermute | solution.py:349
  47.7 5.9 %inner.5 = (f32[2,4096,128]{2,1,0:T(8,128)S(1)}, f32[2,4096,128]{2,1,0:T(8,128)S(1)}, f32[2,544,128]{2,1,0:T(8,128)S(1)}) custom-call(s32[1,512]{1,0:T(1,128)S(1)} %get-tuple-element.41.rows.rows_line, f32[2,544,128]{2,1,0:T(8,128)S(1)} %get-tuple-element.60.entry, bf16[544,640]{1,0:T(8,128)(2,1)S(1)} %get-tuple-element.48.same, ...), custom_call_target="tpu_custom_call", output_to_operand_aliasing={{0}: (8, {})} | custom-call | tf_op jit(solution)/shard_map/inner/pallas_call | solution.py:443
  53.5 0.0 collective-permute-done.11.got_a
  53.6 0.0 collective-permute-done.12.got_b
  53.6 0.0 collective-permute-done.9.got_x
  53.6 0.0 collective-permute-done.10.got_z
  53.6 4.0 %last.1 = (f32[2,4096,128]{2,1,0:T(8,128)S(1)}, f32[2,4096,128]{2,1,0:T(8,128)}) custom-call(s32[1,512]{1,0:T(1,128)S(1)} %get-tuple-element.41.rows.rows_line, f32[2,4096,128]{2,1,0:T(8,128)S(1)} %get-tuple-element.62.stale, f32[2,256,128]{2,1,0:T(8,128)S(1)} %collective-permute-done.9.got_x, ...), custom_call_target="tpu_custom_call", output_to_operand_aliasing={{0}: (1, {})} | custom-call | tf_op jit(solution)/shard_map/last/pallas_call | solution.py:454
  (1 shorter events, 0.0 us)
Async XLA Ops:
  1.5 6.0 %collective-permute-start = (f32[3,256]{1,0:T(4,128)S(1)}, f32[3,256]{1,0:T(4,128)S(1)}, u32[]{:S(2)}, u32[]{:S(2)}) collective-permute-start(f32[3,256]{1,0:T(4,128)S(1)} %pad_maximum_fusion.packed), channel_id=1, source_target_pairs={{0,4},{4,8},{8,12},{12,16},{16,20},{20,24},{24,28},{1,5},{5,9},{9,... | collective-permute-start | bytes 9224 | tf_op jit(solution)/shard_map/ppermute | solution.py:349
  4.7 13.0 %copy-start = (f32[1,256,2048]{2,1,0:T(8,128)S(1)}, f32[1,256,2048]{2,1,0:T(8,128)}, u32[]{:S(2)}) copy-start(f32[1,256,2048]{2,1,0:T(8,128)} %param.6) | copy-start | bytes 6291460
  8.6 17.3 %collective-permute-start.1 = (f32[2,256,128]{2,1,0:T(8,128)S(1)}, f32[2,256,128]{2,1,0:T(8,128)S(1)}, u32[]{:S(2)}, u32[]{:S(2)}) collective-permute-start(f32[2,256,128]{2,1,0:T(8,128)S(1)} %get-tuple-element.42), channel_id=1, source_target_pairs={{0,4},{4,0},{8,12},{12,8},{16,20},{20,16},{24,28},{28,24},{1,5},{5... | collective-permute-start | bytes 786440 | tf_op jit(solution)/shard_map/ppermute | solution.py:349
  8.9 17.1 %collective-permute-start.2 = (f32[2,256,128]{2,1,0:T(8,128)S(1)}, f32[2,256,128]{2,1,0:T(8,128)S(1)}, u32[]{:S(2)}, u32[]{:S(2)}) collective-permute-start(f32[2,256,128]{2,1,0:T(8,128)S(1)} %get-tuple-element.43), channel_id=1, source_target_pairs={{4,8},{8,4},{12,16},{16,12},{20,24},{24,20},{5,9},{9,5},{13,17},{1... | collective-permute-start | bytes 786440 | tf_op jit(solution)/shard_map/ppermute | solution.py:349
  13.1 12.8 %collective-permute-start.3 = (f32[2,16,128]{2,1,0:T(8,128)S(1)}, f32[2,16,128]{2,1,0:T(8,128)S(1)}, u32[]{:S(2)}, u32[]{:S(2)}) collective-permute-start(f32[2,16,128]{2,1,0:T(8,128)S(1)} %get-tuple-element.44), channel_id=1, source_target_pairs={{0,1},{1,0},{2,3},{3,2},{4,5},{5,4},{6,7},{7,6},{8,9},{9,8},{10,11... | collective-permute-start | bytes 49160 | tf_op jit(solution)/shard_map/ppermute | solution.py:349
  14.6 11.3 %collective-permute-start.4 = (f32[2,16,128]{2,1,0:T(8,128)S(1)}, f32[2,16,128]{2,1,0:T(8,128)S(1)}, u32[]{:S(2)}, u32[]{:S(2)}) collective-permute-start(f32[2,16,128]{2,1,0:T(8,128)S(1)} %get-tuple-element.45), channel_id=1, source_target_pairs={{1,2},{2,1},{5,6},{6,5},{9,10},{10,9},{13,14},{14,13},{17,18},{18,... | collective-permute-start | bytes 49160 | tf_op jit(solution)/shard_map/ppermute | solution.py:349
  26.6 13.5 %collective-permute-start.5 = (f32[2,256,128]{2,1,0:T(8,128)S(1)}, f32[2,256,128]{2,1,0:T(8,128)S(1)}, u32[]{:S(2)}, u32[]{:S(2)}) collective-permute-start(f32[2,256,128]{2,1,0:T(8,128)S(1)} %get-tuple-element.53), channel_id=1, source_target_pairs={{0,4},{4,0},{8,12},{12,8},{16,20},{20,16},{24,28},{28,24},{1,5},{5... | collective-permute-start | bytes 786440 | tf_op jit(solution)/shard_map/ppermute | solution.py:349
  26.7 13.5 %collective-permute-start.6 = (f32[2,256,128]{2,1,0:T(8,128)S(1)}, f32[2,256,128]{2,1,0:T(8,128)S(1)}, u32[]{:S(2)}, u32[]{:S(2)}) collective-permute-start(f32[2,256,128]{2,1,0:T(8,128)S(1)} %get-tuple-element.54), channel_id=1, source_target_pairs={{4,8},{8,4},{12,16},{16,12},{20,24},{24,20},{5,9},{9,5},{13,17},{1... | collective-permute-start | bytes 786440 | tf_op jit(solution)/shard_map/ppermute | solution.py:349
  31.1 9.1 %collective-permute-start.7 = (f32[2,16,128]{2,1,0:T(8,128)S(1)}, f32[2,16,128]{2,1,0:T(8,128)S(1)}, u32[]{:S(2)}, u32[]{:S(2)}) collective-permute-start(f32[2,16,128]{2,1,0:T(8,128)S(1)} %get-tuple-element.55), channel_id=1, source_target_pairs={{0,1},{1,0},{2,3},{3,2},{4,5},{5,4},{6,7},{7,6},{8,9},{9,8},{10,11... | collective-permute-start | bytes 49160 | tf_op jit(solution)/shard_map/ppermute | solution.py:349
  31.1 9.0 %collective-permute-start.8 = (f32[2,16,128]{2,1,0:T(8,128)S(1)}, f32[2,16,128]{2,1,0:T(8,128)S(1)}, u32[]{:S(2)}, u32[]{:S(2)}) collective-permute-start(f32[2,16,128]{2,1,0:T(8,128)S(1)} %get-tuple-element.56), channel_id=1, source_target_pairs={{1,2},{2,1},{5,6},{6,5},{9,10},{10,9},{13,14},{14,13},{17,18},{18,... | collective-permute-start | bytes 49160 | tf_op jit(solution)/shard_map/ppermute | solution.py:349
  40.8 12.7 %collective-permute-start.9 = (f32[2,256,128]{2,1,0:T(8,128)S(1)}, f32[2,256,128]{2,1,0:T(8,128)S(1)}, u32[]{:S(2)}, u32[]{:S(2)}) collective-permute-start(f32[2,256,128]{2,1,0:T(8,128)S(1)} %get-tuple-element.63), channel_id=1, source_target_pairs={{0,4},{4,0},{8,12},{12,8},{16,20},{20,16},{24,28},{28,24},{1,5},{5... | collective-permute-start | bytes 786440 | tf_op jit(solution)/shard_map/ppermute | solution.py:349
  40.9 12.7 %collective-permute-start.10 = (f32[2,256,128]{2,1,0:T(8,128)S(1)}, f32[2,256,128]{2,1,0:T(8,128)S(1)}, u32[]{:S(2)}, u32[]{:S(2)}) collective-permute-start(f32[2,256,128]{2,1,0:T(8,128)S(1)} %get-tuple-element.64), channel_id=1, source_target_pairs={{4,8},{8,4},{12,16},{16,12},{20,24},{24,20},{5,9},{9,5},{13,17},{1... | collective-permute-start | bytes 786440 | tf_op jit(solution)/shard_map/ppermute | solution.py:349
  44.5 9.0 %collective-permute-start.11 = (f32[2,16,128]{2,1,0:T(8,128)S(1)}, f32[2,16,128]{2,1,0:T(8,128)S(1)}, u32[]{:S(2)}, u32[]{:S(2)}) collective-permute-start(f32[2,16,128]{2,1,0:T(8,128)S(1)} %get-tuple-element.65), channel_id=1, source_target_pairs={{0,1},{1,0},{2,3},{3,2},{4,5},{5,4},{6,7},{7,6},{8,9},{9,8},{10,11... | collective-permute-start | bytes 49160 | tf_op jit(solution)/shard_map/ppermute | solution.py:349
  44.6 9.0 %collective-permute-start.12 = (f32[2,16,128]{2,1,0:T(8,128)S(1)}, f32[2,16,128]{2,1,0:T(8,128)S(1)}, u32[]{:S(2)}, u32[]{:S(2)}) collective-permute-start(f32[2,16,128]{2,1,0:T(8,128)S(1)} %get-tuple-element.66), channel_id=1, source_target_pairs={{1,2},{2,1},{5,6},{6,5},{9,10},{10,9},{13,14},{14,13},{17,18},{18,... | collective-permute-start | bytes 49160 | tf_op jit(solution)/shard_map/ppermute | solution.py:349

commit v2 on v1

--- a/solution.py
+++ b/solution.py
@@ -1,4 +1,5 @@
 import functools
+import math
 import jax
 import jax.numpy as jnp
 from jax import lax
@@ -8,6 +9,7 @@
 
 ITERS = 3
 LOADS = 4
+GROUP = 2
 OWN_VMEM = 47
 LANES = 128
 SUB = 8
@@ -26,17 +28,20 @@
     return (row // SUB) * (SUB * chunks) + (block % chunks) * SUB + row % SUB
 
 
-def pieces(x):
-    high = x.astype(jnp.bfloat16)
-    low = (x - high.astype(jnp.float32)).astype(jnp.bfloat16)
-    return high, low
-
-
-def summed(same, x):
-    high, low = pieces(x)
-    return jnp.dot(same, high, preferred_element_type=jnp.float32) + jnp.dot(
-        same, low, preferred_element_type=jnp.float32
-    )
+def pieces(x, count):
+    out = []
+    for _ in range(count):
+        out.append(x.astype(jnp.bfloat16))
+        x = x - out[-1].astype(jnp.float32)
+    return out
+
+
+def summed(same, x, count=2):
+    out = None
+    for piece in pieces(x, count):
+        product = jnp.dot(same, piece, preferred_element_type=jnp.float32)
+        out = product if out is None else out + product
+    return out
 
 
 def parity(axis):
@@ -92,26 +97,25 @@
     return copies
 
 
-def own_kernel(packed, displacement, field, entry, stiff, line, staged, scalars, sem, load_sem):
+def own_kernel(packed, displacement, field, entry, stiff, staged, scalars, sem, load_sem):
     loads = load_parts(displacement, field, load_sem, LOADS)
     for copy in loads:
         copy.start()
     listed = into_smem(packed[0:1, :], staged, scalars, sem)
     alive = lax.axis_index("sec") < lax.axis_size("sec") - 1
-    line[...] = packed[2:3, :] * alive.astype(jnp.float32)
-    stiff[...] = columns(line[...])
+    stiff[...] = columns(packed[2:3, :] * alive.astype(jnp.float32))
     listed.wait()
-    for copy in loads:
-        copy.wait()
-
-    def take(slot, row):
-        for part in range(2):
+    for part in range(2):
+        for copy in loads[part * LOADS : (part + 1) * LOADS]:
+            copy.wait()
+
+        def take(slot, row):
             entry[part, pl.ds(slot, 1), :] = field[part, pl.ds(row, 1), :]
 
-    each_slot(packed.shape[1], lambda j: scalars[0, j], take)
-
-
-def first_kernel(chunks, packed, prev, field, own_entry, own_stiff, own_stiff_line, entry, stiff, rows, stiff_line, send_x, send_z, halo_a, halo_b, staged, scalars, taken, sem):
+        each_slot(packed.shape[1], lambda j: scalars[0, j], take)
+
+
+def first_kernel(chunks, packed, prev, field, own_entry, own_stiff, entry, stiff, rows, send_x, send_z, halo_a, halo_b, staged, scalars, taken, sem):
     blocks = field.shape[1]
     matches = own_entry.shape[1]
     count = 2 * matches
@@ -120,9 +124,8 @@
     line = prev[2:3, :] * (lax.axis_index("sec") > 0).astype(jnp.float32)
     stiff_prev = columns(line)
     own_rows, prev_rows = packed[0:1, :].astype(jnp.int32), prev[1:2, :].astype(jnp.int32)
-    for out, first, second in ((rows, own_rows, prev_rows), (stiff_line, own_stiff_line[...], line)):
-        out[:, :matches] = jnp.where(even, first, second)
-        out[:, matches:] = jnp.where(even, second, first)
+    rows[:, :matches] = jnp.where(even, own_rows, prev_rows)
+    rows[:, matches:] = jnp.where(even, prev_rows, own_rows)
     for part in range(2):
         for chunk in range(chunks):
             entry[part, pl.ds(count + chunk, 1), :] = field[part, pl.ds(chunk * SUB, 1), :]
@@ -156,7 +159,7 @@
         place(own_entry, own_stiff[...], matches, send_z)
 
 
-def setup_kernel(chunks, rows, rows_line, stiff_line, spring, same, weight, factor, picked, column):
+def setup_kernel(chunks, rows, rows_line, stiff, spring, same, weight, factor, picked, column):
     blocks = spring.shape[0]
     count = rows_line.shape[1]
     total = count + 2 * chunks
@@ -172,14 +175,11 @@
     def band(step, carry):
         at = pl.ds(pl.multiple_of(step * 32, 32), 32)
         col = column[at, :]
-        total_stiff = jnp.zeros((32, LANES), jnp.float32)
         for piece in range(count // LANES):
             cut = slice(piece * LANES, (piece + 1) * LANES)
             equal = col == rows_line[:, cut].astype(jnp.float32)
             same[at, cut] = equal.astype(jnp.float32).astype(jnp.bfloat16)
-            total_stiff += jnp.where(equal, stiff_line[:, cut], 0.0)
         same[at, count:] = (col == edge_line).astype(jnp.float32).astype(jnp.bfloat16)
-        factor[at, :] = jnp.broadcast_to(jnp.sum(total_stiff, axis=1, keepdims=True), (32, LANES))
         return carry
 
     lax.fori_loop(0, total // 32, band, 0)
@@ -192,7 +192,7 @@
         take(count + chunk, chunk * SUB)
         take(count + chunks + chunk, chunk * SUB + last)
     spring_here = picked[...]
-    inverse = 1.0 / (4.0 * spring_here + factor[...])
+    inverse = 1.0 / (4.0 * spring_here + summed(same[:, :count], stiff[...], 3))
     weight[...] = 4.0 * spring_here * inverse
     factor[...] = 0.8 * inverse
 
@@ -225,7 +225,7 @@
             before, here = here, after
 
 
-def bulk(chunks, rows, field, entry, same, stiff, weight, factor, nearby, base):
+def bulk(chunks, rows, field, nearby, base):
     blocks = field.shape[1]
     span = SUB * chunks
     strips = blocks // span
@@ -233,12 +233,14 @@
     stencil(field, nearby, 0, chunks, top=True)
     stencil(field, nearby, blocks - span, chunks, bottom=True)
 
-    def pair(step, carry):
-        for inner in range(2):
-            stencil(field, nearby, pl.multiple_of((1 + step * 2 + inner) * span, SUB), chunks)
+    group = math.gcd(strips - 2, GROUP)
+
+    def some(step, carry):
+        for inner in range(group):
+            stencil(field, nearby, pl.multiple_of((1 + step * group + inner) * span, SUB), chunks)
         return carry
 
-    lax.fori_loop(0, (strips - 2) // 2, pair, 0)
+    lax.fori_loop(0, (strips - 2) // group, some, 0)
 
     def take(slot, row):
         for part in range(2):
@@ -248,15 +250,6 @@
     for chunk in range(chunks):
         take(count + chunk, chunk * SUB)
         take(count + chunks + chunk, blocks - span + chunk * SUB + SUB - 1)
-    own = jnp.concatenate([entry[part, :count, :] * stiff[...] for part in range(2)], axis=1)
-    total = summed(same[:, :count], own)
-    for part in range(2):
-        value = entry[part]
-        base[part] = (
-            value
-            + weight[...] * (base[part] - value)
-            - factor[...] * total[:, part * LANES : (part + 1) * LANES]
-        )
 
 
 def halo_rows(got_a, got_b):
@@ -279,11 +272,11 @@
                 field[part, at, :] = field[part, at, :] + halo[chunk : chunk + 1, :]
 
 
-def inner_kernel(chunks, rows, entry, same, stiff, weight, factor, field, nearby, base):
-    bulk(chunks, rows, field, entry, same, stiff, weight, factor, nearby, base)
-
-
-def scatter_inner_kernel(chunks, rows, entry, same, stiff, weight, factor, got_a, got_b, stale, field, nearby, base):
+def inner_kernel(chunks, rows, field, nearby, base):
+    bulk(chunks, rows, field, nearby, base)
+
+
+def scatter_inner_kernel(chunks, rows, entry, got_a, got_b, stale, field, nearby, base):
     add_halo(field, halo_rows(got_a, got_b), chunks)
 
     def put(slot, row):
@@ -291,13 +284,24 @@
             field[part, pl.ds(row, 1), :] = entry[part, pl.ds(slot, 1), :]
 
     each_slot(rows.shape[1], lambda j: rows[0, j], put)
-    bulk(chunks, rows, field, entry, same, stiff, weight, factor, nearby, base)
-
-
-def new_entries(got_x, got_z, halos, base, same, weight, factor):
-    count = 2 * got_x.shape[1]
-    got = jnp.concatenate(
-        [jnp.concatenate([got_x[part], got_z[part]], axis=0) for part in range(2)], axis=1
+    bulk(chunks, rows, field, nearby, base)
+
+
+def new_entries(got_x, got_z, halos, entry, base, same, weight, factor, stiff):
+    matches = got_x.shape[1]
+    count = 2 * matches
+    term = jnp.concatenate(
+        [
+            jnp.concatenate(
+                [
+                    got[part] - stiff[at : at + matches, :] * entry[part, at : at + matches, :]
+                    for at, got in ((0, got_x), (matches, got_z))
+                ],
+                axis=0,
+            )
+            for part in range(2)
+        ],
+        axis=1,
     )
     unused = same.shape[1] - count - 2 * halos[0][0].shape[0]
     edges = jnp.concatenate(
@@ -307,30 +311,35 @@
         ],
         axis=1,
     )
-    total = summed(same[:, :count], got)
+    total = summed(same[:, :count], term)
     outside = summed(same[:, count:], edges)
     out = []
     for part in range(2):
         cut = slice(part * LANES, (part + 1) * LANES)
-        out.append(base[part] + weight[...] * outside[:, cut] + factor[...] * total[:, cut])
+        value = entry[part]
+        out.append(
+            value
+            + weight[...] * ((base[part] - value) + outside[:, cut])
+            + factor[...] * total[:, cut]
+        )
     return out
 
 
-def step_kernel(chunks, got_x, got_z, got_a, got_b, base, same, weight, factor, stiff, entry, send_x, send_z, halo_a, halo_b):
+def step_kernel(chunks, got_x, got_z, got_a, got_b, old, base, same, weight, factor, stiff, entry, send_x, send_z, halo_a, halo_b):
     matches = got_x.shape[1]
     count = 2 * matches
     halos = halo_rows(got_a, got_b)
-    for part, value in enumerate(new_entries(got_x, got_z, halos, base, same, weight, factor)):
+    for part, value in enumerate(new_entries(got_x, got_z, halos, old, base, same, weight, factor, stiff)):
         entry[part] = value
         send_x[part] = value[:matches] * stiff[:matches, :]
         send_z[part] = value[matches:count] * stiff[matches:, :]
     send_edges(entry, halo_a, halo_b, count, chunks)
 
 
-def last_kernel(chunks, rows, stale, got_x, got_z, got_a, got_b, base, same, weight, factor, nearby, out, entry, sem):
+def last_kernel(chunks, rows, stale, got_x, got_z, got_a, got_b, old, base, same, weight, factor, stiff, nearby, out, entry, sem):
     halos = halo_rows(got_a, got_b)
     add_halo(nearby, halos, chunks)
-    for part, value in enumerate(new_entries(got_x, got_z, halos, base, same, weight, factor)):
+    for part, value in enumerate(new_entries(got_x, got_z, halos, old, base, same, weight, factor, stiff)):
         entry[part] = value
     stores = load_parts(nearby, out, sem, LOADS)
     for part in range(2):
@@ -404,22 +413,22 @@
         pltpu.VMEM((1, matches), jnp.int32),
         pltpu.SMEM((1, matches), jnp.int32),
     ]
-    field, own_entry, own_stiff, own_stiff_line = call(
+    field, own_entry, own_stiff = call(
         "own",
         own_kernel,
         [VM, HBM],
-        [big, send, (VM, f32(matches, LANES)), (VM, f32(1, matches))],
+        [big, send, (VM, f32(matches, LANES))],
         scratch_shapes=staging + [pltpu.SemaphoreType.DMA, pltpu.SemaphoreType.DMA((2 * LOADS,))],
         vmem=OWN_VMEM << 20,
     )(packed, tiled(displacement[:, 0]))
-    entry, stiff, rows, stiff_line, send_x, send_z, halo_a, halo_b = call(
+    entry, stiff, rows, send_x, send_z, halo_a, halo_b = call(
         "first",
         functools.partial(first_kernel, chunks),
-        [VM] * 6,
-        [entries, (VM, f32(count, LANES)), rows_shape, (VM, f32(1, count)), send, send, halo, halo],
+        [VM] * 5,
+        [entries, (VM, f32(count, LANES)), rows_shape, send, send, halo, halo],
         scratch_shapes=staging
         + [pltpu.VMEM((fields, matches, LANES), jnp.float32), pltpu.SemaphoreType.DMA],
-    )(packed, prev, field, own_entry, own_stiff, own_stiff_line)
+    )(packed, prev, field, own_entry, own_stiff)
 
     for sweep in range(ITERS):
         if sweep > 0:
@@ -435,33 +444,33 @@
                 [SM, VM, VM, VM],
                 [(VM, jax.ShapeDtypeStruct((total, count + LANES), jnp.bfloat16)), wide, wide],
                 scratch_shapes=[pltpu.VMEM((total, LANES), jnp.float32)] * 2,
-            )(rows, rows, stiff_line, tiled(spring[0]))
+            )(rows, rows, stiff, tiled(spring[0]))
             nearby, base = call(
-                "inner", functools.partial(inner_kernel, chunks), [SM] + [VM] * 6, [big, entries]
-            )(rows, entry, same, stiff, weight, factor, field)
+                "inner", functools.partial(inner_kernel, chunks), [SM, VM], [big, entries]
+            )(rows, field)
         else:
             field, nearby, base = call(
                 "inner",
                 functools.partial(scatter_inner_kernel, chunks),
-                [SM] + [VM] * 8,
+                [SM] + [VM] * 4,
                 [big, big, entries],
-                input_output_aliases={8: 0},
-            )(rows, entry, same, stiff, weight, factor, *past, nearby)
+                input_output_aliases={4: 0},
+            )(rows, entry, *past, nearby)
         if sweep < ITERS - 1:
             entry, send_x, send_z, halo_a, halo_b = call(
-                "step", functools.partial(step_kernel, chunks), [VM] * 9, [entries, send, send, halo, halo]
-            )(got_x, got_z, got_a, got_b, base, same, weight, factor, stiff)
+                "step", functools.partial(step_kernel, chunks), [VM] * 10, [entries, send, send, halo, halo]
+            )(got_x, got_z, got_a, got_b, entry, base, same, weight, factor, stiff)
     _, out = call(
         "last",
         functools.partial(last_kernel, chunks),
-        [SM] + [VM] * 9,
+        [SM] + [VM] * 11,
         [big, (HBM, f32(fields, blocks, LANES))],
         scratch_shapes=[
             pltpu.VMEM((fields, total, LANES), jnp.float32),
             pltpu.SemaphoreType.DMA((2 * LOADS,)),
         ],
         input_output_aliases={1: 0},
-    )(rows, nearby, got_x, got_z, got_a, got_b, base, same, weight, factor)
+    )(rows, nearby, got_x, got_z, got_a, got_b, entry, base, same, weight, factor, stiff)
     return untiled(out)[:, None]
 
 

time: 57.8 us -> 56.6 us (0.979)
  Pallas kernels: 29.1 us -> 27 us
    pallas_call x2, Pallas kernels: 11.8 us -> 10.9 us  [on_device(): call('inner', functools.partial(scatter_inner_kernel, chunks), [SM] + [VM...]
    pallas_call x1, Pallas kernels: 3 us -> 2.22 us  [on_device(): call('setup', functools.partial(setup_kernel, chunks), [SM, VM, VM, VM],...]
  transfers between devices with their start and end apart: 13 -> 13, of which waited for: 0 -> 1; matrix products, arithmetic and copies ran while one was open for 0% -> 0% of each run, Pallas kernels for 40% -> 36%
where the time goes in v2:
time: 56.6 us; the launch traced here: 56.1 us
  Pallas kernels  27 us (48%)
  starting transfers between devices  26.8 us (47%)
  other arithmetic  1.49 us (3%)
    ppermute x13, starting transfers between devices, exchange(): return lax.ppermute(array, axis, pairs)  26.8 us
    pallas_call x2, Pallas kernels, on_device(): call('inner', functools.partial(scatter_inner_kernel, chunks), [SM] + [VM...  10.9 us
    pallas_call x1, Pallas kernels, on_device(): call('inner', functools.partial(inner_kernel, chunks), [SM, VM], [big, en...  4.72 us
    pallas_call x1, Pallas kernels, on_device(): call('last', functools.partial(last_kernel, chunks), [SM] + [VM] * 11, [b...  4.05 us
    pallas_call x1, Pallas kernels, on_device(): call('own', own_kernel, [VM, HBM], [big, send, (VM, f32(matches, LANES))]...  2.54 us
    pallas_call x1, Pallas kernels, on_device(): call('setup', functools.partial(setup_kernel, chunks), [SM, VM, VM, VM],...  2.22 us
    pallas_call x2, Pallas kernels, on_device(): call('step', functools.partial(step_kernel, chunks), [VM] * 10, [entries,...  1.46 us
  transfers between devices with their start and end apart: 13, of which 1 were waited for; matrix products, arithmetic and copies ran while one was open for 0% of the time, Pallas kernels for 36%

profile of v2, /device:TPU:3, one launch (start us, length us, event | category | flops | bytes accessed | tf_op | source)
XLA Modules:
  0.0 56.1 jit_solution(8790615725172135113)
XLA Ops:
  0.0 0.7 %fusion.3 = f32[2,256]{1,0:T(2,128)S(1)} fusion(s32[2,1,256]{2,1,0:T(1,128)} %param.8), kind=kLoop, calls=%fused_computation.18 | loop fusion | flops 22016 | bytes 4096 | tf_op jit(solution)/shard_map/convert_element_type | solution.py:409
  0.7 0.8 %select_reduce_fusion = f32[256]{0:T(256)S(1)} fusion(f32[8]{0:T(128)} %param.7, s32[256]{0:T(256)} %bitcast.36), kind=kLoop, calls=%fused_computation | loop fusion | flops 5888 | bytes 2080 | tf_op jit(solution)/shard_map/reduce_sum | solution.py:408
  1.5 3.2 %collective-permute-start = (f32[3,256]{1,0:T(4,128)S(1)}, f32[3,256]{1,0:T(4,128)S(1)}, u32[]{:S(2)}, u32[]{:S(2)}) collective-permute-start(f32[3,256]{1,0:T(4,128)S(1)} %pad_maximum_fusion.packed), channel_id=1, source_target_pairs={{0,4},{4,8},{8,12},{12,16},{16,20},{20,24},{24,28},{1,5},{5,9},{9,... | collective-permute-start | bytes 9224 | tf_op jit(solution)/shard_map/ppermute | solution.py:358
  4.7 2.5 %own.1 = (f32[2,4096,128]{2,1,0:T(8,128)S(1)}, f32[2,256,128]{2,1,0:T(8,128)S(1)}, f32[256,128]{1,0:T(8,128)S(1)}) custom-call(f32[3,256]{1,0:T(4,128)S(1)} %pad_maximum_fusion.packed, f32[2,4096,128]{2,1,0:T(8,128)} %bitcast.34), custom_call_target="tpu_custom_call" | custom-call | tf_op jit(solution)/shard_map/own/pallas_call | solution.py:416
  7.2 0.0 collective-permute-done.prev
  7.2 0.0 copy-start
  7.2 1.1 %first.1 = (f32[2,544,128]{2,1,0:T(8,128)S(1)}, f32[512,128]{1,0:T(8,128)S(1)}, s32[1,512]{1,0:T(1,128)S(1)}, f32[2,256,128]{2,1,0:T(8,128)S(1)}, f32[2,256,128]...) custom-call(f32[3,256]{1,0:T(4,128)S(1)} %pad_maximum_fusion.packed, ...), custom_call_target="tpu_custom_call" | custom-call | tf_op jit(solution)/shard_map/first/pallas_call | solution.py:424
  8.4 0.3 collective-permute-start.1
  8.6 4.2 %collective-permute-start.2 = (f32[2,256,128]{2,1,0:T(8,128)S(1)}, f32[2,256,128]{2,1,0:T(8,128)S(1)}, u32[]{:S(2)}, u32[]{:S(2)}) collective-permute-start(f32[2,256,128]{2,1,0:T(8,128)S(1)} %get-tuple-element.40), channel_id=1, source_target_pairs={{4,8},{8,4},{12,16},{16,12},{20,24},{24,20},{5,9},{9,5},{13,17},{1... | collective-permute-start | bytes 786440 | tf_op jit(solution)/shard_map/ppermute | solution.py:358
  12.8 1.6 %collective-permute-start.3 = (f32[2,16,128]{2,1,0:T(8,128)S(1)}, f32[2,16,128]{2,1,0:T(8,128)S(1)}, u32[]{:S(2)}, u32[]{:S(2)}) collective-permute-start(f32[2,16,128]{2,1,0:T(8,128)S(1)} %get-tuple-element.41), channel_id=1, source_target_pairs={{0,1},{1,0},{2,3},{3,2},{4,5},{5,4},{6,7},{7,6},{8,9},{9,8},{10,11... | collective-permute-start | bytes 49160 | tf_op jit(solution)/shard_map/ppermute | solution.py:358
  14.4 3.0 %collective-permute-start.4 = (f32[2,16,128]{2,1,0:T(8,128)S(1)}, f32[2,16,128]{2,1,0:T(8,128)S(1)}, u32[]{:S(2)}, u32[]{:S(2)}) collective-permute-start(f32[2,16,128]{2,1,0:T(8,128)S(1)} %get-tuple-element.42), channel_id=1, source_target_pairs={{1,2},{2,1},{5,6},{6,5},{9,10},{10,9},{13,14},{14,13},{17,18},{18,... | collective-permute-start | bytes 49160 | tf_op jit(solution)/shard_map/ppermute | solution.py:358
  17.4 4.7 %inner.3 = (f32[2,4096,128]{2,1,0:T(8,128)S(1)}, f32[2,544,128]{2,1,0:T(8,128)S(1)}) custom-call(s32[1,512]{1,0:T(1,128)S(1)} %get-tuple-element.38.rows.rows_line, f32[2,4096,128]{2,1,0:T(8,128)S(1)} %get-tuple-element.35.field), custom_call_target="tpu_custom_call" | custom-call | tf_op jit(solution)/shard_map/inner/pallas_call | solution.py:448
  22.2 0.0 copy-done
  22.2 2.2 %setup.1 = (bf16[544,640]{1,0:T(8,128)(2,1)S(1)}, f32[544,128]{1,0:T(8,128)S(1)}, f32[544,128]{1,0:T(8,128)S(1)}) custom-call(s32[1,512]{1,0:T(1,128)S(1)} %get-tuple-element.38.rows.rows_line, s32[1,512]{1,0:T(1,128)S(1)} %get-tuple-element.38.rows.rows_line, f32[512,128]{1,0:T(8,128)S(1)} %get-tuple-element.45.stiff, f32[4096,128]{1,0:T(8,128)S(1)} %bitcast.33), custom_call_target="tpu_custom_call" | custom-call | tf_op jit(solution)/shard_map/setup/pallas_call | solution.py:441
  24.4 0.0 collective-permute-done.3.got_a
  24.4 0.0 collective-permute-done.4.got_b
  24.4 0.0 collective-permute-done.1.got_x
  24.4 0.0 collective-permute-done.2.got_z
  24.5 0.7 %step.2 = (f32[2,544,128]{2,1,0:T(8,128)S(1)}, f32[2,256,128]{2,1,0:T(8,128)S(1)}, f32[2,256,128]{2,1,0:T(8,128)S(1)}, f32[2,16,128]{2,1,0:T(8,128)S(1)}, f32[2,16,128]{2,1,0:T(8,128)S(1)}) custom-call(f32[2,256,128]{2,1,0:T(8,128)S(1)} %collective-permute-done.1.got_x, f32[2,256,128]{2,1,0:T(8,128)S(1)} %collective-permute-done.2.got_z, ...), custom_call_target="tpu_custom_call" | custom-call | tf_op jit(solution)/shard_map/step/pallas_call | solution.py:460
  25.2 0.1 collective-permute-start.5
  25.3 4.4 %collective-permute-start.6 = (f32[2,256,128]{2,1,0:T(8,128)S(1)}, f32[2,256,128]{2,1,0:T(8,128)S(1)}, u32[]{:S(2)}, u32[]{:S(2)}) collective-permute-start(f32[2,256,128]{2,1,0:T(8,128)S(1)} %get-tuple-element.50), channel_id=1, source_target_pairs={{4,8},{8,4},{12,16},{16,12},{20,24},{24,20},{5,9},{9,5},{13,17},{1... | collective-permute-start | bytes 786440 | tf_op jit(solution)/shard_map/ppermute | solution.py:358
  29.6 0.1 collective-permute-start.7
  29.7 3.1 %collective-permute-start.8 = (f32[2,16,128]{2,1,0:T(8,128)S(1)}, f32[2,16,128]{2,1,0:T(8,128)S(1)}, u32[]{:S(2)}, u32[]{:S(2)}) collective-permute-start(f32[2,16,128]{2,1,0:T(8,128)S(1)} %get-tuple-element.52), channel_id=1, source_target_pairs={{1,2},{2,1},{5,6},{6,5},{9,10},{10,9},{13,14},{14,13},{17,18},{18,... | collective-permute-start | bytes 49160 | tf_op jit(solution)/shard_map/ppermute | solution.py:358
  32.8 5.4 %inner.4 = (f32[2,4096,128]{2,1,0:T(8,128)S(1)}, f32[2,4096,128]{2,1,0:T(8,128)S(1)}, f32[2,544,128]{2,1,0:T(8,128)S(1)}) custom-call(s32[1,512]{1,0:T(1,128)S(1)} %get-tuple-element.38.rows.rows_line, f32[2,544,128]{2,1,0:T(8,128)S(1)} %get-tuple-element.53.entry.old, ...), custom_call_target="tpu_custom_call", output_to_operand_aliasing={{0}: (4, {})} | custom-call | tf_op jit(solution)/shard_map/inner/pallas_call | solution.py:452
  38.2 0.0 collective-permute-done.7.got_a
  38.2 0.0 collective-permute-done.8.got_b
  38.2 0.0 collective-permute-done.5.got_x
  38.3 0.0 collective-permute-done.6.got_z
  38.3 0.7 %step.3 = (f32[2,544,128]{2,1,0:T(8,128)S(1)}, f32[2,256,128]{2,1,0:T(8,128)S(1)}, f32[2,256,128]{2,1,0:T(8,128)S(1)}, f32[2,16,128]{2,1,0:T(8,128)S(1)}, f32[2,16,128]{2,1,0:T(8,128)S(1)}) custom-call(f32[2,256,128]{2,1,0:T(8,128)S(1)} %collective-permute-done.5.got_x, f32[2,256,128]{2,1,0:T(8,128)S(1)} %collective-permute-done.6.got_z, ...), custom_call_target="tpu_custom_call" | custom-call | tf_op jit(solution)/shard_map/step/pallas_call | solution.py:460
  39.0 0.1 collective-permute-start.9
  39.1 3.8 %collective-permute-start.10 = (f32[2,256,128]{2,1,0:T(8,128)S(1)}, f32[2,256,128]{2,1,0:T(8,128)S(1)}, u32[]{:S(2)}, u32[]{:S(2)}) collective-permute-start(f32[2,256,128]{2,1,0:T(8,128)S(1)} %get-tuple-element.60), channel_id=1, source_target_pairs={{4,8},{8,4},{12,16},{16,12},{20,24},{24,20},{5,9},{9,5},{13,17},{1... | collective-permute-start | bytes 786440 | tf_op jit(solution)/shard_map/ppermute | solution.py:358
  42.9 0.1 collective-permute-start.11
  43.0 3.1 %collective-permute-start.12 = (f32[2,16,128]{2,1,0:T(8,128)S(1)}, f32[2,16,128]{2,1,0:T(8,128)S(1)}, u32[]{:S(2)}, u32[]{:S(2)}) collective-permute-start(f32[2,16,128]{2,1,0:T(8,128)S(1)} %get-tuple-element.62), channel_id=1, source_target_pairs={{1,2},{2,1},{5,6},{6,5},{9,10},{10,9},{13,14},{14,13},{17,18},{18,... | collective-permute-start | bytes 49160 | tf_op jit(solution)/shard_map/ppermute | solution.py:358
  46.1 5.4 %inner.5 = (f32[2,4096,128]{2,1,0:T(8,128)S(1)}, f32[2,4096,128]{2,1,0:T(8,128)S(1)}, f32[2,544,128]{2,1,0:T(8,128)S(1)}) custom-call(s32[1,512]{1,0:T(1,128)S(1)} %get-tuple-element.38.rows.rows_line, f32[2,544,128]{2,1,0:T(8,128)S(1)} %get-tuple-element.56.entry.old, ...), custom_call_target="tpu_custom_call", output_to_operand_aliasing={{0}: (4, {})} | custom-call | tf_op jit(solution)/shard_map/inner/pallas_call | solution.py:452
  51.5 0.0 collective-permute-done.11.got_a
  51.5 0.0 collective-permute-done.12.got_b
  51.5 0.5 collective-permute-done.9.got_x
  52.0 0.0 collective-permute-done.10.got_z
  52.0 4.0 %last.1 = (f32[2,4096,128]{2,1,0:T(8,128)S(1)}, f32[2,4096,128]{2,1,0:T(8,128)}) custom-call(s32[1,512]{1,0:T(1,128)S(1)} %get-tuple-element.38.rows.rows_line, f32[2,4096,128]{2,1,0:T(8,128)S(1)} %get-tuple-element.58.stale, f32[2,256,128]{2,1,0:T(8,128)S(1)} %collective-permute-done.9.got_x, ...), custom_call_target="tpu_custom_call", output_to_operand_aliasing={{0}: (1, {})} | custom-call | tf_op jit(solution)/shard_map/last/pallas_call | solution.py:463
  (1 shorter events, 0.0 us)
Async XLA Ops:
  1.5 5.7 %collective-permute-start = (f32[3,256]{1,0:T(4,128)S(1)}, f32[3,256]{1,0:T(4,128)S(1)}, u32[]{:S(2)}, u32[]{:S(2)}) collective-permute-start(f32[3,256]{1,0:T(4,128)S(1)} %pad_maximum_fusion.packed), channel_id=1, source_target_pairs={{0,4},{4,8},{8,12},{12,16},{16,20},{20,24},{24,28},{1,5},{5,9},{9,... | collective-permute-start | bytes 9224 | tf_op jit(solution)/shard_map/ppermute | solution.py:358
  7.2 14.9 %copy-start = (f32[1,256,2048]{2,1,0:T(8,128)S(1)}, f32[1,256,2048]{2,1,0:T(8,128)}, u32[]{:S(2)}) copy-start(f32[1,256,2048]{2,1,0:T(8,128)} %param.6) | copy-start | bytes 6291460
  8.4 16.1 %collective-permute-start.1 = (f32[2,256,128]{2,1,0:T(8,128)S(1)}, f32[2,256,128]{2,1,0:T(8,128)S(1)}, u32[]{:S(2)}, u32[]{:S(2)}) collective-permute-start(f32[2,256,128]{2,1,0:T(8,128)S(1)} %get-tuple-element.39), channel_id=1, source_target_pairs={{0,4},{4,0},{8,12},{12,8},{16,20},{20,16},{24,28},{28,24},{1,5},{5... | collective-permute-start | bytes 786440 | tf_op jit(solution)/shard_map/ppermute | solution.py:358
  8.6 15.8 %collective-permute-start.2 = (f32[2,256,128]{2,1,0:T(8,128)S(1)}, f32[2,256,128]{2,1,0:T(8,128)S(1)}, u32[]{:S(2)}, u32[]{:S(2)}) collective-permute-start(f32[2,256,128]{2,1,0:T(8,128)S(1)} %get-tuple-element.40), channel_id=1, source_target_pairs={{4,8},{8,4},{12,16},{16,12},{20,24},{24,20},{5,9},{9,5},{13,17},{1... | collective-permute-start | bytes 786440 | tf_op jit(solution)/shard_map/ppermute | solution.py:358
  12.8 11.6 %collective-permute-start.3 = (f32[2,16,128]{2,1,0:T(8,128)S(1)}, f32[2,16,128]{2,1,0:T(8,128)S(1)}, u32[]{:S(2)}, u32[]{:S(2)}) collective-permute-start(f32[2,16,128]{2,1,0:T(8,128)S(1)} %get-tuple-element.41), channel_id=1, source_target_pairs={{0,1},{1,0},{2,3},{3,2},{4,5},{5,4},{6,7},{7,6},{8,9},{9,8},{10,11... | collective-permute-start | bytes 49160 | tf_op jit(solution)/shard_map/ppermute | solution.py:358
  14.4 10.0 %collective-permute-start.4 = (f32[2,16,128]{2,1,0:T(8,128)S(1)}, f32[2,16,128]{2,1,0:T(8,128)S(1)}, u32[]{:S(2)}, u32[]{:S(2)}) collective-permute-start(f32[2,16,128]{2,1,0:T(8,128)S(1)} %get-tuple-element.42), channel_id=1, source_target_pairs={{1,2},{2,1},{5,6},{6,5},{9,10},{10,9},{13,14},{14,13},{17,18},{18,... | collective-permute-start | bytes 49160 | tf_op jit(solution)/shard_map/ppermute | solution.py:358
  25.2 13.1 %collective-permute-start.5 = (f32[2,256,128]{2,1,0:T(8,128)S(1)}, f32[2,256,128]{2,1,0:T(8,128)S(1)}, u32[]{:S(2)}, u32[]{:S(2)}) collective-permute-start(f32[2,256,128]{2,1,0:T(8,128)S(1)} %get-tuple-element.49), channel_id=1, source_target_pairs={{0,4},{4,0},{8,12},{12,8},{16,20},{20,16},{24,28},{28,24},{1,5},{5... | collective-permute-start | bytes 786440 | tf_op jit(solution)/shard_map/ppermute | solution.py:358
  25.3 13.0 %collective-permute-start.6 = (f32[2,256,128]{2,1,0:T(8,128)S(1)}, f32[2,256,128]{2,1,0:T(8,128)S(1)}, u32[]{:S(2)}, u32[]{:S(2)}) collective-permute-start(f32[2,256,128]{2,1,0:T(8,128)S(1)} %get-tuple-element.50), channel_id=1, source_target_pairs={{4,8},{8,4},{12,16},{16,12},{20,24},{24,20},{5,9},{9,5},{13,17},{1... | collective-permute-start | bytes 786440 | tf_op jit(solution)/shard_map/ppermute | solution.py:358
  29.6 8.6 %collective-permute-start.7 = (f32[2,16,128]{2,1,0:T(8,128)S(1)}, f32[2,16,128]{2,1,0:T(8,128)S(1)}, u32[]{:S(2)}, u32[]{:S(2)}) collective-permute-start(f32[2,16,128]{2,1,0:T(8,128)S(1)} %get-tuple-element.51), channel_id=1, source_target_pairs={{0,1},{1,0},{2,3},{3,2},{4,5},{5,4},{6,7},{7,6},{8,9},{9,8},{10,11... | collective-permute-start | bytes 49160 | tf_op jit(solution)/shard_map/ppermute | solution.py:358
  29.7 8.5 %collective-permute-start.8 = (f32[2,16,128]{2,1,0:T(8,128)S(1)}, f32[2,16,128]{2,1,0:T(8,128)S(1)}, u32[]{:S(2)}, u32[]{:S(2)}) collective-permute-start(f32[2,16,128]{2,1,0:T(8,128)S(1)} %get-tuple-element.52), channel_id=1, source_target_pairs={{1,2},{2,1},{5,6},{6,5},{9,10},{10,9},{13,14},{14,13},{17,18},{18,... | collective-permute-start | bytes 49160 | tf_op jit(solution)/shard_map/ppermute | solution.py:358
  39.0 13.0 %collective-permute-start.9 = (f32[2,256,128]{2,1,0:T(8,128)S(1)}, f32[2,256,128]{2,1,0:T(8,128)S(1)}, u32[]{:S(2)}, u32[]{:S(2)}) collective-permute-start(f32[2,256,128]{2,1,0:T(8,128)S(1)} %get-tuple-element.59), channel_id=1, source_target_pairs={{0,4},{4,0},{8,12},{12,8},{16,20},{20,16},{24,28},{28,24},{1,5},{5... | collective-permute-start | bytes 786440 | tf_op jit(solution)/shard_map/ppermute | solution.py:358
  39.1 13.0 %collective-permute-start.10 = (f32[2,256,128]{2,1,0:T(8,128)S(1)}, f32[2,256,128]{2,1,0:T(8,128)S(1)}, u32[]{:S(2)}, u32[]{:S(2)}) collective-permute-start(f32[2,256,128]{2,1,0:T(8,128)S(1)} %get-tuple-element.60), channel_id=1, source_target_pairs={{4,8},{8,4},{12,16},{16,12},{20,24},{24,20},{5,9},{9,5},{13,17},{1... | collective-permute-start | bytes 786440 | tf_op jit(solution)/shard_map/ppermute | solution.py:358
  42.9 8.6 %collective-permute-start.11 = (f32[2,16,128]{2,1,0:T(8,128)S(1)}, f32[2,16,128]{2,1,0:T(8,128)S(1)}, u32[]{:S(2)}, u32[]{:S(2)}) collective-permute-start(f32[2,16,128]{2,1,0:T(8,128)S(1)} %get-tuple-element.61), channel_id=1, source_target_pairs={{0,1},{1,0},{2,3},{3,2},{4,5},{5,4},{6,7},{7,6},{8,9},{9,8},{10,11... | collective-permute-start | bytes 49160 | tf_op jit(solution)/shard_map/ppermute | solution.py:358
  43.0 8.5 %collective-permute-start.12 = (f32[2,16,128]{2,1,0:T(8,128)S(1)}, f32[2,16,128]{2,1,0:T(8,128)S(1)}, u32[]{:S(2)}, u32[]{:S(2)}) collective-permute-start(f32[2,16,128]{2,1,0:T(8,128)S(1)} %get-tuple-element.62), channel_id=1, source_target_pairs={{1,2},{2,1},{5,6},{6,5},{9,10},{10,9},{13,14},{14,13},{17,18},{18,... | collective-permute-start | bytes 49160 | tf_op jit(solution)/shard_map/ppermute | solution.py:358

commit v3 on v2

--- a/solution.py
+++ b/solution.py
@@ -24,8 +24,9 @@
 
 
 def tile_row(block, chunks):
-    row = block // chunks
-    return (row // SUB) * (SUB * chunks) + (block % chunks) * SUB + row % SUB
+    bits, low = chunks.bit_length() - 1, SUB.bit_length() - 1
+    row = block >> bits
+    return ((row >> low) << (bits + low)) | ((block & (chunks - 1)) << low) | (row & (SUB - 1))
 
 
 def pieces(x, count):
@@ -68,16 +69,16 @@
 
 def each_slot(count, rows, body):
     def some(step, carry):
-        for inner in range(8):
-            slot = step * 8 + inner
+        for inner in range(16):
+            slot = step * 16 + inner
             body(slot, rows(slot))
         return carry
 
-    lax.fori_loop(0, count // 8, some, 0)
+    lax.fori_loop(0, count // 16, some, 0)
 
 
 def into_smem(line, staged, scalars, sem):
-    staged[...] = line.astype(jnp.int32)
+    staged[...] = line
     copy = pltpu.make_async_copy(staged, scalars, sem)
     copy.start()
     return copy
@@ -97,13 +98,18 @@
     return copies
 
 
-def own_kernel(packed, displacement, field, entry, stiff, staged, scalars, sem, load_sem):
+def coupling_of(classes, table, alive):
+    out = jnp.zeros(classes.shape, jnp.float32)
+    for level in range(table.shape[1]):
+        out = jnp.where(classes == level, table[:, level : level + 1], out)
+    return out * alive.astype(jnp.float32)
+
+
+def own_kernel(chunks, packed, displacement, field, entry, staged, scalars, sem, load_sem):
     loads = load_parts(displacement, field, load_sem, LOADS)
     for copy in loads:
         copy.start()
-    listed = into_smem(packed[0:1, :], staged, scalars, sem)
-    alive = lax.axis_index("sec") < lax.axis_size("sec") - 1
-    stiff[...] = columns(packed[2:3, :] * alive.astype(jnp.float32))
+    listed = into_smem(tile_row(packed[0], chunks), staged, scalars, sem)
     listed.wait()
     for part in range(2):
         for copy in loads[part * LOADS : (part + 1) * LOADS]:
@@ -112,18 +118,19 @@
         def take(slot, row):
             entry[part, pl.ds(slot, 1), :] = field[part, pl.ds(row, 1), :]
 
-        each_slot(packed.shape[1], lambda j: scalars[0, j], take)
-
-
-def first_kernel(chunks, packed, prev, field, own_entry, own_stiff, entry, stiff, rows, send_x, send_z, halo_a, halo_b, staged, scalars, taken, sem):
+        each_slot(packed.shape[2], lambda j: scalars[0, j], take)
+
+
+def first_kernel(chunks, table, packed, prev, field, own_entry, entry, stiff, rows, send_x, send_z, halo_a, halo_b, staged, scalars, taken, sem):
     blocks = field.shape[1]
     matches = own_entry.shape[1]
     count = 2 * matches
-    listed = into_smem(prev[1:2, :], staged, scalars, sem)
+    own_rows, prev_rows = tile_row(packed[0], chunks), tile_row(prev[1], chunks)
+    listed = into_smem(prev_rows, staged, scalars, sem)
     even = parity("sec") == 0
-    line = prev[2:3, :] * (lax.axis_index("sec") > 0).astype(jnp.float32)
-    stiff_prev = columns(line)
-    own_rows, prev_rows = packed[0:1, :].astype(jnp.int32), prev[1:2, :].astype(jnp.int32)
+    section = lax.axis_index("sec")
+    stiff_own = columns(coupling_of(packed[2], table, section < lax.axis_size("sec") - 1))
+    stiff_prev = columns(coupling_of(prev[2], table, section > 0))
     rows[:, :matches] = jnp.where(even, own_rows, prev_rows)
     rows[:, matches:] = jnp.where(even, prev_rows, own_rows)
     for part in range(2):
@@ -150,13 +157,13 @@
 
     @pl.when(even)
     def _():
-        place(own_entry, own_stiff[...], 0, send_x)
+        place(own_entry, stiff_own, 0, send_x)
         place(taken, stiff_prev, matches, send_z)
 
     @pl.when(jnp.logical_not(even))
     def _():
         place(taken, stiff_prev, 0, send_x)
-        place(own_entry, own_stiff[...], matches, send_z)
+        place(own_entry, stiff_own, matches, send_z)
 
 
 def setup_kernel(chunks, rows, rows_line, stiff, spring, same, weight, factor, picked, column):
@@ -404,20 +411,17 @@
     wide = (VM, f32(total, LANES))
     rows_shape = (VM, jax.ShapeDtypeStruct((1, count), jnp.int32))
 
-    level = jnp.arange(stiff_table.shape[0], dtype=jnp.int32)[:, None]
-    coupling = jnp.sum(jnp.where(match_class == level, stiff_table[:, None], 0.0), axis=0, keepdims=True)
-    places = tile_row(match_blocks[:, 0], chunks).astype(jnp.float32)
-    packed = jnp.concatenate([places, coupling], axis=0)
+    packed = jnp.concatenate([match_blocks, match_class[:, None]], axis=0)
     prev = exchange(packed, "sec", [(i, i + 1) for i in range(sections - 1)])
     staging = [
         pltpu.VMEM((1, matches), jnp.int32),
         pltpu.SMEM((1, matches), jnp.int32),
     ]
-    field, own_entry, own_stiff = call(
+    field, own_entry = call(
         "own",
-        own_kernel,
+        functools.partial(own_kernel, chunks),
         [VM, HBM],
-        [big, send, (VM, f32(matches, LANES))],
+        [big, send],
         scratch_shapes=staging + [pltpu.SemaphoreType.DMA, pltpu.SemaphoreType.DMA((2 * LOADS,))],
         vmem=OWN_VMEM << 20,
     )(packed, tiled(displacement[:, 0]))
@@ -428,7 +432,7 @@
         [entries, (VM, f32(count, LANES)), rows_shape, send, send, halo, halo],
         scratch_shapes=staging
         + [pltpu.VMEM((fields, matches, LANES), jnp.float32), pltpu.SemaphoreType.DMA],
-    )(packed, prev, field, own_entry, own_stiff)
+    )(stiff_table[None], packed, prev, field, own_entry)
 
     for sweep in range(ITERS):
         if sweep > 0:

time: 56.6 us -> 56 us (0.989)
  Pallas kernels: 27 us -> 25.9 us
  waiting for transfers between devices: 0.55 us -> 1.37 us
  other arithmetic: 1.49 us -> 0.71 us
    ppermute x13, waiting for transfers between devices: 0.55 us -> 1.37 us  [exchange(): return lax.ppermute(array, axis, pairs)]
    reduce_sum x1 -> x0, other arithmetic: 0.78 us -> none  [on_device(): jnp.sum(jnp.where(match_class == level, stiff_table[:, None], 0.0), axis=...]
    convert_element_type x1 -> x0, other arithmetic: 0.7 us -> none  [on_device(): places = tile_row(match_blocks[:, 0], chunks).astype(jnp.float32)]
    concatenate x1, other arithmetic: 0.01 us -> 0.71 us  [on_device(): packed = jnp.concatenate([match_blocks, match_class[:, None]], axis=0)]
  transfers between devices with their start and end apart: 13 -> 13, of which waited for: 1 -> 1; matrix products, arithmetic and copies ran while one was open for 0% -> 0% of each run, Pallas kernels for 36% -> 35%
where the time goes in v3:
time: 56 us; the launch traced here: 55.4 us
  starting transfers between devices  27.1 us (48%)
  Pallas kernels  25.9 us (46%)
  waiting for transfers between devices  1.37 us (2%)
  other arithmetic  0.71 us (1%)
    ppermute x13, starting transfers between devices, exchange(): return lax.ppermute(array, axis, pairs)  27.1 us
    pallas_call x2, Pallas kernels, on_device(): call('inner', functools.partial(scatter_inner_kernel, chunks), [SM] + [VM...  10.4 us
    pallas_call x1, Pallas kernels, on_device(): call('inner', functools.partial(inner_kernel, chunks), [SM, VM], [big, en...  4.56 us
    pallas_call x1, Pallas kernels, on_device(): call('last', functools.partial(last_kernel, chunks), [SM] + [VM] * 11, [b...  3.93 us
    pallas_call x1, Pallas kernels, on_device(): call('own', functools.partial(own_kernel, chunks), [VM, HBM], [big, send]...  2.49 us
    pallas_call x1, Pallas kernels, on_device(): call('setup', functools.partial(setup_kernel, chunks), [SM, VM, VM, VM],...  2.09 us
    pallas_call x2, Pallas kernels, on_device(): call('step', functools.partial(step_kernel, chunks), [VM] * 10, [entries,...  1.45 us
    ppermute x13, waiting for transfers between devices, exchange(): return lax.ppermute(array, axis, pairs)  1.37 us
  transfers between devices with their start and end apart: 13, of which 1 were waited for; matrix products, arithmetic and copies ran while one was open for 0% of the time, Pallas kernels for 35%

profile of v3, /device:TPU:3, one launch (start us, length us, event | category | flops | bytes accessed | tf_op | source)
XLA Modules:
  0.0 55.4 jit_solution(2091258538406667307)
XLA Ops:
  0.0 0.0 copy-start.1
  0.0 0.7 %pad_add_fusion.packed = s32[3,1,256]{2,1,0:T(1,128)S(1)} fusion(s32[1,1,256]{2,1,0:T(1,128)} %bitcast.20, s32[2,1,256]{2,1,0:T(1,128)} %param.8), kind=kLoop, calls=%fused_computation | loop fusion | flops 768 | bytes 6144 | tf_op jit(solution)/shard_map/concatenate | solution.py:414
  0.7 3.2 %collective-permute-start = (s32[3,1,256]{2,1,0:T(1,128)S(1)}, s32[3,1,256]{2,1,0:T(1,128)S(1)}, u32[]{:S(2)}, u32[]{:S(2)}) collective-permute-start(s32[3,1,256]{2,1,0:T(1,128)S(1)} %pad_add_fusion.packed), channel_id=1, source_target_pairs={{0,4},{4,8},{8,12},{12,16},{16,20},{20,24},{24,28},{1,5},{5,9},{9,... | collective-permute-start | bytes 9224 | tf_op jit(solution)/shard_map/ppermute | solution.py:365
  3.9 2.5 %own.1 = (f32[2,4096,128]{2,1,0:T(8,128)S(1)}, f32[2,256,128]{2,1,0:T(8,128)S(1)}) custom-call(s32[3,1,256]{2,1,0:T(1,128)S(1)} %pad_add_fusion.packed, f32[2,4096,128]{2,1,0:T(8,128)} %bitcast.19), custom_call_target="tpu_custom_call" | custom-call | tf_op jit(solution)/shard_map/own/pallas_call | solution.py:420
  6.4 0.0 collective-permute-done.prev
  6.4 0.0 copy-done.1
  6.4 0.0 copy-start
  6.4 1.1 %first.1 = (f32[2,544,128]{2,1,0:T(8,128)S(1)}, f32[512,128]{1,0:T(8,128)S(1)}, s32[1,512]{1,0:T(1,128)S(1)}, f32[2,256,128]{2,1,0:T(8,128)S(1)}, f32[2,256,128]...) custom-call(f32[1,8]{1,0:T(1,128)S(1)} %bitcast.18, s32[3,1,256]{2,1,0:T(1,128)S(1)} %pad_add_fusion.packed, ...), custom_call_target="tpu_custom_call" | custom-call | tf_op jit(solution)/shard_map/first/pallas_call | solution.py:428
  7.5 0.3 collective-permute-start.1
  7.7 4.2 %collective-permute-start.2 = (f32[2,256,128]{2,1,0:T(8,128)S(1)}, f32[2,256,128]{2,1,0:T(8,128)S(1)}, u32[]{:S(2)}, u32[]{:S(2)}) collective-permute-start(f32[2,256,128]{2,1,0:T(8,128)S(1)} %get-tuple-element.38), channel_id=1, source_target_pairs={{4,8},{8,4},{12,16},{16,12},{20,24},{24,20},{5,9},{9,5},{13,17},{1... | collective-permute-start | bytes 786440 | tf_op jit(solution)/shard_map/ppermute | solution.py:365
  11.9 1.6 %collective-permute-start.3 = (f32[2,16,128]{2,1,0:T(8,128)S(1)}, f32[2,16,128]{2,1,0:T(8,128)S(1)}, u32[]{:S(2)}, u32[]{:S(2)}) collective-permute-start(f32[2,16,128]{2,1,0:T(8,128)S(1)} %get-tuple-element.39), channel_id=1, source_target_pairs={{0,1},{1,0},{2,3},{3,2},{4,5},{5,4},{6,7},{7,6},{8,9},{9,8},{10,11... | collective-permute-start | bytes 49160 | tf_op jit(solution)/shard_map/ppermute | solution.py:365
  13.5 3.0 %collective-permute-start.4 = (f32[2,16,128]{2,1,0:T(8,128)S(1)}, f32[2,16,128]{2,1,0:T(8,128)S(1)}, u32[]{:S(2)}, u32[]{:S(2)}) collective-permute-start(f32[2,16,128]{2,1,0:T(8,128)S(1)} %get-tuple-element.40), channel_id=1, source_target_pairs={{1,2},{2,1},{5,6},{6,5},{9,10},{10,9},{13,14},{14,13},{17,18},{18,... | collective-permute-start | bytes 49160 | tf_op jit(solution)/shard_map/ppermute | solution.py:365
  16.6 4.6 %inner.3 = (f32[2,4096,128]{2,1,0:T(8,128)S(1)}, f32[2,544,128]{2,1,0:T(8,128)S(1)}) custom-call(s32[1,512]{1,0:T(1,128)S(1)} %get-tuple-element.36.rows.rows_line, f32[2,4096,128]{2,1,0:T(8,128)S(1)} %get-tuple-element.34.field), custom_call_target="tpu_custom_call" | custom-call | tf_op jit(solution)/shard_map/inner/pallas_call | solution.py:452
  21.1 0.0 copy-done
  21.2 2.1 %setup.1 = (bf16[544,640]{1,0:T(8,128)(2,1)S(1)}, f32[544,128]{1,0:T(8,128)S(1)}, f32[544,128]{1,0:T(8,128)S(1)}) custom-call(s32[1,512]{1,0:T(1,128)S(1)} %get-tuple-element.36.rows.rows_line, s32[1,512]{1,0:T(1,128)S(1)} %get-tuple-element.36.rows.rows_line, f32[512,128]{1,0:T(8,128)S(1)} %get-tuple-element.43.stiff, f32[4096,128]{1,0:T(8,128)S(1)} %bitcast.17), custom_call_target="tpu_custom_call" | custom-call | tf_op jit(solution)/shard_map/setup/pallas_call | solution.py:445
  23.3 0.0 collective-permute-done.3.got_a
  23.3 0.0 collective-permute-done.4.got_b
  23.3 0.0 collective-permute-done.1.got_x
  23.3 0.0 collective-permute-done.2.got_z
  23.3 0.7 %step.2 = (f32[2,544,128]{2,1,0:T(8,128)S(1)}, f32[2,256,128]{2,1,0:T(8,128)S(1)}, f32[2,256,128]{2,1,0:T(8,128)S(1)}, f32[2,16,128]{2,1,0:T(8,128)S(1)}, f32[2,16,128]{2,1,0:T(8,128)S(1)}) custom-call(f32[2,256,128]{2,1,0:T(8,128)S(1)} %collective-permute-done.1.got_x, f32[2,256,128]{2,1,0:T(8,128)S(1)} %collective-permute-done.2.got_z, ...), custom_call_target="tpu_custom_call" | custom-call | tf_op jit(solution)/shard_map/step/pallas_call | solution.py:464
  24.0 0.1 collective-permute-start.5
  24.1 4.4 %collective-permute-start.6 = (f32[2,256,128]{2,1,0:T(8,128)S(1)}, f32[2,256,128]{2,1,0:T(8,128)S(1)}, u32[]{:S(2)}, u32[]{:S(2)}) collective-permute-start(f32[2,256,128]{2,1,0:T(8,128)S(1)} %get-tuple-element.48), channel_id=1, source_target_pairs={{4,8},{8,4},{12,16},{16,12},{20,24},{24,20},{5,9},{9,5},{13,17},{1... | collective-permute-start | bytes 786440 | tf_op jit(solution)/shard_map/ppermute | solution.py:365
  28.5 0.1 collective-permute-start.7
  28.5 3.1 %collective-permute-start.8 = (f32[2,16,128]{2,1,0:T(8,128)S(1)}, f32[2,16,128]{2,1,0:T(8,128)S(1)}, u32[]{:S(2)}, u32[]{:S(2)}) collective-permute-start(f32[2,16,128]{2,1,0:T(8,128)S(1)} %get-tuple-element.50), channel_id=1, source_target_pairs={{1,2},{2,1},{5,6},{6,5},{9,10},{10,9},{13,14},{14,13},{17,18},{18,... | collective-permute-start | bytes 49160 | tf_op jit(solution)/shard_map/ppermute | solution.py:365
  31.6 5.2 %inner.4 = (f32[2,4096,128]{2,1,0:T(8,128)S(1)}, f32[2,4096,128]{2,1,0:T(8,128)S(1)}, f32[2,544,128]{2,1,0:T(8,128)S(1)}) custom-call(s32[1,512]{1,0:T(1,128)S(1)} %get-tuple-element.36.rows.rows_line, f32[2,544,128]{2,1,0:T(8,128)S(1)} %get-tuple-element.51.entry.old, ...), custom_call_target="tpu_custom_call", output_to_operand_aliasing={{0}: (4, {})} | custom-call | tf_op jit(solution)/shard_map/inner/pallas_call | solution.py:456
  36.8 0.0 collective-permute-done.7.got_a
  36.8 0.0 collective-permute-done.8.got_b
  36.8 0.0 collective-permute-done.5.got_x
  36.8 0.0 collective-permute-done.6.got_z
  36.8 0.7 %step.3 = (f32[2,544,128]{2,1,0:T(8,128)S(1)}, f32[2,256,128]{2,1,0:T(8,128)S(1)}, f32[2,256,128]{2,1,0:T(8,128)S(1)}, f32[2,16,128]{2,1,0:T(8,128)S(1)}, f32[2,16,128]{2,1,0:T(8,128)S(1)}) custom-call(f32[2,256,128]{2,1,0:T(8,128)S(1)} %collective-permute-done.5.got_x, f32[2,256,128]{2,1,0:T(8,128)S(1)} %collective-permute-done.6.got_z, ...), custom_call_target="tpu_custom_call" | custom-call | tf_op jit(solution)/shard_map/step/pallas_call | solution.py:464
  37.6 0.1 collective-permute-start.9
  37.7 4.3 %collective-permute-start.10 = (f32[2,256,128]{2,1,0:T(8,128)S(1)}, f32[2,256,128]{2,1,0:T(8,128)S(1)}, u32[]{:S(2)}, u32[]{:S(2)}) collective-permute-start(f32[2,256,128]{2,1,0:T(8,128)S(1)} %get-tuple-element.58), channel_id=1, source_target_pairs={{4,8},{8,4},{12,16},{16,12},{20,24},{24,20},{5,9},{9,5},{13,17},{1... | collective-permute-start | bytes 786440 | tf_op jit(solution)/shard_map/ppermute | solution.py:365
  42.0 0.4 collective-permute-start.11
  42.4 2.5 %collective-permute-start.12 = (f32[2,16,128]{2,1,0:T(8,128)S(1)}, f32[2,16,128]{2,1,0:T(8,128)S(1)}, u32[]{:S(2)}, u32[]{:S(2)}) collective-permute-start(f32[2,16,128]{2,1,0:T(8,128)S(1)} %get-tuple-element.60), channel_id=1, source_target_pairs={{1,2},{2,1},{5,6},{6,5},{9,10},{10,9},{13,14},{14,13},{17,18},{18,... | collective-permute-start | bytes 49160 | tf_op jit(solution)/shard_map/ppermute | solution.py:365
  44.9 5.2 %inner.5 = (f32[2,4096,128]{2,1,0:T(8,128)S(1)}, f32[2,4096,128]{2,1,0:T(8,128)S(1)}, f32[2,544,128]{2,1,0:T(8,128)S(1)}) custom-call(s32[1,512]{1,0:T(1,128)S(1)} %get-tuple-element.36.rows.rows_line, f32[2,544,128]{2,1,0:T(8,128)S(1)} %get-tuple-element.54.entry.old, ...), custom_call_target="tpu_custom_call", output_to_operand_aliasing={{0}: (4, {})} | custom-call | tf_op jit(solution)/shard_map/inner/pallas_call | solution.py:456
  50.1 0.0 collective-permute-done.11.got_a
  50.1 0.0 collective-permute-done.12.got_b
  50.1 1.3 %collective-permute-done.9.got_x = f32[2,256,128]{2,1,0:T(8,128)S(1)} collective-permute-done((f32[2,256,128]{2,1,0:T(8,128)S(1)}, f32[2,256,128]{2,1,0:T(8,128)S(1)}, u32[]{:S(2)}, u32[]{:S(2)}) %collective-permute-start.9) | collective-permute-done | bytes 262176 | tf_op jit(solution)/shard_map/ppermute | solution.py:365
  51.4 0.0 collective-permute-done.10.got_z
  51.4 3.9 %last.1 = (f32[2,4096,128]{2,1,0:T(8,128)S(1)}, f32[2,4096,128]{2,1,0:T(8,128)}) custom-call(s32[1,512]{1,0:T(1,128)S(1)} %get-tuple-element.36.rows.rows_line, f32[2,4096,128]{2,1,0:T(8,128)S(1)} %get-tuple-element.56.stale, f32[2,256,128]{2,1,0:T(8,128)S(1)} %collective-permute-done.9.got_x, ...), custom_call_target="tpu_custom_call", output_to_operand_aliasing={{0}: (1, {})} | custom-call | tf_op jit(solution)/shard_map/last/pallas_call | solution.py:467
Async XLA Ops:
  0.0 6.4 %copy-start.1 = (f32[8]{0:T(128)S(1)}, f32[8]{0:T(128)}, u32[]{:S(2)}) copy-start(f32[8]{0:T(128)} %param.7) | copy-start | bytes 100
  0.7 5.7 %collective-permute-start = (s32[3,1,256]{2,1,0:T(1,128)S(1)}, s32[3,1,256]{2,1,0:T(1,128)S(1)}, u32[]{:S(2)}, u32[]{:S(2)}) collective-permute-start(s32[3,1,256]{2,1,0:T(1,128)S(1)} %pad_add_fusion.packed), channel_id=1, source_target_pairs={{0,4},{4,8},{8,12},{12,16},{16,20},{20,24},{24,28},{1,5},{5,9},{9,... | collective-permute-start | bytes 9224 | tf_op jit(solution)/shard_map/ppermute | solution.py:365
  6.4 14.7 %copy-start = (f32[1,256,2048]{2,1,0:T(8,128)S(1)}, f32[1,256,2048]{2,1,0:T(8,128)}, u32[]{:S(2)}) copy-start(f32[1,256,2048]{2,1,0:T(8,128)} %param.6) | copy-start | bytes 6291460
  7.5 15.8 %collective-permute-start.1 = (f32[2,256,128]{2,1,0:T(8,128)S(1)}, f32[2,256,128]{2,1,0:T(8,128)S(1)}, u32[]{:S(2)}, u32[]{:S(2)}) collective-permute-start(f32[2,256,128]{2,1,0:T(8,128)S(1)} %get-tuple-element.37), channel_id=1, source_target_pairs={{0,4},{4,0},{8,12},{12,8},{16,20},{20,16},{24,28},{28,24},{1,5},{5... | collective-permute-start | bytes 786440 | tf_op jit(solution)/shard_map/ppermute | solution.py:365
  7.7 15.5 %collective-permute-start.2 = (f32[2,256,128]{2,1,0:T(8,128)S(1)}, f32[2,256,128]{2,1,0:T(8,128)S(1)}, u32[]{:S(2)}, u32[]{:S(2)}) collective-permute-start(f32[2,256,128]{2,1,0:T(8,128)S(1)} %get-tuple-element.38), channel_id=1, source_target_pairs={{4,8},{8,4},{12,16},{16,12},{20,24},{24,20},{5,9},{9,5},{13,17},{1... | collective-permute-start | bytes 786440 | tf_op jit(solution)/shard_map/ppermute | solution.py:365
  11.9 11.3 %collective-permute-start.3 = (f32[2,16,128]{2,1,0:T(8,128)S(1)}, f32[2,16,128]{2,1,0:T(8,128)S(1)}, u32[]{:S(2)}, u32[]{:S(2)}) collective-permute-start(f32[2,16,128]{2,1,0:T(8,128)S(1)} %get-tuple-element.39), channel_id=1, source_target_pairs={{0,1},{1,0},{2,3},{3,2},{4,5},{5,4},{6,7},{7,6},{8,9},{9,8},{10,11... | collective-permute-start | bytes 49160 | tf_op jit(solution)/shard_map/ppermute | solution.py:365
  13.5 9.7 %collective-permute-start.4 = (f32[2,16,128]{2,1,0:T(8,128)S(1)}, f32[2,16,128]{2,1,0:T(8,128)S(1)}, u32[]{:S(2)}, u32[]{:S(2)}) collective-permute-start(f32[2,16,128]{2,1,0:T(8,128)S(1)} %get-tuple-element.40), channel_id=1, source_target_pairs={{1,2},{2,1},{5,6},{6,5},{9,10},{10,9},{13,14},{14,13},{17,18},{18,... | collective-permute-start | bytes 49160 | tf_op jit(solution)/shard_map/ppermute | solution.py:365
  24.0 12.8 %collective-permute-start.5 = (f32[2,256,128]{2,1,0:T(8,128)S(1)}, f32[2,256,128]{2,1,0:T(8,128)S(1)}, u32[]{:S(2)}, u32[]{:S(2)}) collective-permute-start(f32[2,256,128]{2,1,0:T(8,128)S(1)} %get-tuple-element.47), channel_id=1, source_target_pairs={{0,4},{4,0},{8,12},{12,8},{16,20},{20,16},{24,28},{28,24},{1,5},{5... | collective-permute-start | bytes 786440 | tf_op jit(solution)/shard_map/ppermute | solution.py:365
  24.1 12.7 %collective-permute-start.6 = (f32[2,256,128]{2,1,0:T(8,128)S(1)}, f32[2,256,128]{2,1,0:T(8,128)S(1)}, u32[]{:S(2)}, u32[]{:S(2)}) collective-permute-start(f32[2,256,128]{2,1,0:T(8,128)S(1)} %get-tuple-element.48), channel_id=1, source_target_pairs={{4,8},{8,4},{12,16},{16,12},{20,24},{24,20},{5,9},{9,5},{13,17},{1... | collective-permute-start | bytes 786440 | tf_op jit(solution)/shard_map/ppermute | solution.py:365
  28.5 8.3 %collective-permute-start.7 = (f32[2,16,128]{2,1,0:T(8,128)S(1)}, f32[2,16,128]{2,1,0:T(8,128)S(1)}, u32[]{:S(2)}, u32[]{:S(2)}) collective-permute-start(f32[2,16,128]{2,1,0:T(8,128)S(1)} %get-tuple-element.49), channel_id=1, source_target_pairs={{0,1},{1,0},{2,3},{3,2},{4,5},{5,4},{6,7},{7,6},{8,9},{9,8},{10,11... | collective-permute-start | bytes 49160 | tf_op jit(solution)/shard_map/ppermute | solution.py:365
  28.5 8.3 %collective-permute-start.8 = (f32[2,16,128]{2,1,0:T(8,128)S(1)}, f32[2,16,128]{2,1,0:T(8,128)S(1)}, u32[]{:S(2)}, u32[]{:S(2)}) collective-permute-start(f32[2,16,128]{2,1,0:T(8,128)S(1)} %get-tuple-element.50), channel_id=1, source_target_pairs={{1,2},{2,1},{5,6},{6,5},{9,10},{10,9},{13,14},{14,13},{17,18},{18,... | collective-permute-start | bytes 49160 | tf_op jit(solution)/shard_map/ppermute | solution.py:365
  37.6 13.9 %collective-permute-start.9 = (f32[2,256,128]{2,1,0:T(8,128)S(1)}, f32[2,256,128]{2,1,0:T(8,128)S(1)}, u32[]{:S(2)}, u32[]{:S(2)}) collective-permute-start(f32[2,256,128]{2,1,0:T(8,128)S(1)} %get-tuple-element.57), channel_id=1, source_target_pairs={{0,4},{4,0},{8,12},{12,8},{16,20},{20,16},{24,28},{28,24},{1,5},{5... | collective-permute-start | bytes 786440 | tf_op jit(solution)/shard_map/ppermute | solution.py:365
  37.7 13.8 %collective-permute-start.10 = (f32[2,256,128]{2,1,0:T(8,128)S(1)}, f32[2,256,128]{2,1,0:T(8,128)S(1)}, u32[]{:S(2)}, u32[]{:S(2)}) collective-permute-start(f32[2,256,128]{2,1,0:T(8,128)S(1)} %get-tuple-element.58), channel_id=1, source_target_pairs={{4,8},{8,4},{12,16},{16,12},{20,24},{24,20},{5,9},{9,5},{13,17},{1... | collective-permute-start | bytes 786440 | tf_op jit(solution)/shard_map/ppermute | solution.py:365
  42.0 8.1 %collective-permute-start.11 = (f32[2,16,128]{2,1,0:T(8,128)S(1)}, f32[2,16,128]{2,1,0:T(8,128)S(1)}, u32[]{:S(2)}, u32[]{:S(2)}) collective-permute-start(f32[2,16,128]{2,1,0:T(8,128)S(1)} %get-tuple-element.59), channel_id=1, source_target_pairs={{0,1},{1,0},{2,3},{3,2},{4,5},{5,4},{6,7},{7,6},{8,9},{9,8},{10,11... | collective-permute-start | bytes 49160 | tf_op jit(solution)/shard_map/ppermute | solution.py:365
  42.4 7.7 %collective-permute-start.12 = (f32[2,16,128]{2,1,0:T(8,128)S(1)}, f32[2,16,128]{2,1,0:T(8,128)S(1)}, u32[]{:S(2)}, u32[]{:S(2)}) collective-permute-start(f32[2,16,128]{2,1,0:T(8,128)S(1)} %get-tuple-element.60), channel_id=1, source_target_pairs={{1,2},{2,1},{5,6},{6,5},{9,10},{10,9},{13,14},{14,13},{17,18},{18,... | collective-permute-start | bytes 49160 | tf_op jit(solution)/shard_map/ppermute | solution.py:365

commit v4 on v3

--- a/solution.py
+++ b/solution.py
@@ -9,7 +9,7 @@
 
 ITERS = 3
 LOADS = 4
-GROUP = 2
+GROUP = 6
 OWN_VMEM = 47
 LANES = 128
 SUB = 8
@@ -166,8 +166,7 @@
         place(own_entry, stiff_own, matches, send_z)
 
 
-def setup_kernel(chunks, rows, rows_line, stiff, spring, same, weight, factor, picked, column):
-    blocks = spring.shape[0]
+def relate(rows_line, stiff, picked, column, same, weight, factor, chunks, blocks):
     count = rows_line.shape[1]
     total = count + 2 * chunks
     last = blocks - SUB * chunks + SUB - 1
@@ -190,14 +189,6 @@
         return carry
 
     lax.fori_loop(0, total // 32, band, 0)
-
-    def take(slot, row):
-        picked[pl.ds(slot, 1), :] = spring[pl.ds(row, 1), :]
-
-    each_slot(count, lambda j: rows[0, j], take)
-    for chunk in range(chunks):
-        take(count + chunk, chunk * SUB)
-        take(count + chunks + chunk, chunk * SUB + last)
     spring_here = picked[...]
     inverse = 1.0 / (4.0 * spring_here + summed(same[:, :count], stiff[...], 3))
     weight[...] = 4.0 * spring_here * inverse
@@ -232,14 +223,12 @@
             before, here = here, after
 
 
-def bulk(chunks, rows, field, nearby, base):
+def strips_all(chunks, field, nearby):
     blocks = field.shape[1]
     span = SUB * chunks
     strips = blocks // span
-    count = rows.shape[1]
     stencil(field, nearby, 0, chunks, top=True)
     stencil(field, nearby, blocks - span, chunks, bottom=True)
-
     group = math.gcd(strips - 2, GROUP)
 
     def some(step, carry):
@@ -249,14 +238,13 @@
 
     lax.fori_loop(0, (strips - 2) // group, some, 0)
 
-    def take(slot, row):
-        for part in range(2):
-            base[part, pl.ds(slot, 1), :] = nearby[part, pl.ds(row, 1), :]
-
+
+def each_entry(chunks, rows, blocks, take):
+    count = rows.shape[1]
     each_slot(count, lambda j: rows[0, j], take)
     for chunk in range(chunks):
         take(count + chunk, chunk * SUB)
-        take(count + chunks + chunk, blocks - span + chunk * SUB + SUB - 1)
+        take(count + chunks + chunk, blocks - SUB * chunks + chunk * SUB + SUB - 1)
 
 
 def halo_rows(got_a, got_b):
@@ -279,29 +267,61 @@
                 field[part, at, :] = field[part, at, :] + halo[chunk : chunk + 1, :]
 
 
-def inner_kernel(chunks, rows, field, nearby, base):
-    bulk(chunks, rows, field, nearby, base)
-
-
-def scatter_inner_kernel(chunks, rows, entry, got_a, got_b, stale, field, nearby, base):
-    add_halo(field, halo_rows(got_a, got_b), chunks)
-
+def start_kernel(chunks, rows, rows_line, stiff, spring, field, nearby, base, same, weight, factor, picked, column):
+    strips_all(chunks, field, nearby)
+
+    def take(slot, row):
+        picked[pl.ds(slot, 1), :] = spring[pl.ds(row, 1), :]
+        for part in range(2):
+            base[part, pl.ds(slot, 1), :] = nearby[part, pl.ds(row, 1), :]
+
+    each_entry(chunks, rows, field.shape[1], take)
+    relate(rows_line, stiff, picked, column, same, weight, factor, chunks, field.shape[1])
+
+
+def scatter_inner_kernel(chunks, rows, entry, stale, field, nearby, base):
     def put(slot, row):
         for part in range(2):
             field[part, pl.ds(row, 1), :] = entry[part, pl.ds(slot, 1), :]
 
     each_slot(rows.shape[1], lambda j: rows[0, j], put)
-    bulk(chunks, rows, field, nearby, base)
-
-
-def new_entries(got_x, got_z, halos, entry, base, same, weight, factor, stiff):
+    strips_all(chunks, field, nearby)
+
+    def take(slot, row):
+        for part in range(2):
+            base[part, pl.ds(slot, 1), :] = nearby[part, pl.ds(row, 1), :]
+
+    each_entry(chunks, rows, field.shape[1], take)
+
+
+def settle_kernel(chunks, got_a, got_b, entry, raw, same, weight, factor, stiff, stale, nearby, base):
+    count = stiff.shape[0]
+    halos = halo_rows(got_a, got_b)
+    add_halo(nearby, halos, chunks)
+    unused = same.shape[1] - count - 2 * chunks
+    edges = jnp.concatenate(
+        [
+            jnp.concatenate([above, below, jnp.zeros((unused, LANES), jnp.float32)], axis=0)
+            for above, below in halos
+        ],
+        axis=1,
+    )
+    outside = summed(same[:, count:], edges)
+    for part in range(2):
+        value = entry[part]
+        base[part] = value + weight[...] * (
+            (raw[part] - value) + outside[:, part * LANES : (part + 1) * LANES]
+        )
+
+
+def new_entries(got_x, got_z, old, base, same, factor, stiff):
     matches = got_x.shape[1]
     count = 2 * matches
     term = jnp.concatenate(
         [
             jnp.concatenate(
                 [
-                    got[part] - stiff[at : at + matches, :] * entry[part, at : at + matches, :]
+                    got[part] - stiff[at : at + matches, :] * old[part, at : at + matches, :]
                     for at, got in ((0, got_x), (matches, got_z))
                 ],
                 axis=0,
@@ -310,43 +330,22 @@
         ],
         axis=1,
     )
-    unused = same.shape[1] - count - 2 * halos[0][0].shape[0]
-    edges = jnp.concatenate(
-        [
-            jnp.concatenate([above, below, jnp.zeros((unused, LANES), jnp.float32)], axis=0)
-            for above, below in halos
-        ],
-        axis=1,
-    )
     total = summed(same[:, :count], term)
-    outside = summed(same[:, count:], edges)
-    out = []
-    for part in range(2):
-        cut = slice(part * LANES, (part + 1) * LANES)
-        value = entry[part]
-        out.append(
-            value
-            + weight[...] * ((base[part] - value) + outside[:, cut])
-            + factor[...] * total[:, cut]
-        )
-    return out
-
-
-def step_kernel(chunks, got_x, got_z, got_a, got_b, old, base, same, weight, factor, stiff, entry, send_x, send_z, halo_a, halo_b):
+    return [base[part] + factor[...] * total[:, part * LANES : (part + 1) * LANES] for part in range(2)]
+
+
+def step_kernel(chunks, got_x, got_z, old, base, same, factor, stiff, entry, send_x, send_z, halo_a, halo_b):
     matches = got_x.shape[1]
     count = 2 * matches
-    halos = halo_rows(got_a, got_b)
-    for part, value in enumerate(new_entries(got_x, got_z, halos, old, base, same, weight, factor, stiff)):
+    for part, value in enumerate(new_entries(got_x, got_z, old, base, same, factor, stiff)):
         entry[part] = value
         send_x[part] = value[:matches] * stiff[:matches, :]
         send_z[part] = value[matches:count] * stiff[matches:, :]
     send_edges(entry, halo_a, halo_b, count, chunks)
 
 
-def last_kernel(chunks, rows, stale, got_x, got_z, got_a, got_b, old, base, same, weight, factor, stiff, nearby, out, entry, sem):
-    halos = halo_rows(got_a, got_b)
-    add_halo(nearby, halos, chunks)
-    for part, value in enumerate(new_entries(got_x, got_z, halos, old, base, same, weight, factor, stiff)):
+def last_kernel(rows, stale, got_x, got_z, old, base, same, factor, stiff, nearby, out, entry, sem):
+    for part, value in enumerate(new_entries(got_x, got_z, old, base, same, factor, stiff)):
         entry[part] = value
     stores = load_parts(nearby, out, sem, LOADS)
     for part in range(2):
@@ -435,46 +434,48 @@
     )(stiff_table[None], packed, prev, field, own_entry)
 
     for sweep in range(ITERS):
-        if sweep > 0:
-            past = (got_a, got_b)
         got_x = exchange(send_x, "sec", near)
         got_z = exchange(send_z, "sec", far)
         got_a = exchange(halo_a, "tile", near_tile)
         got_b = exchange(halo_b, "tile", far_tile)
         if sweep == 0:
-            same, weight, factor = call(
-                "setup",
-                functools.partial(setup_kernel, chunks),
-                [SM, VM, VM, VM],
-                [(VM, jax.ShapeDtypeStruct((total, count + LANES), jnp.bfloat16)), wide, wide],
+            nearby, base, same, weight, factor = call(
+                "start",
+                functools.partial(start_kernel, chunks),
+                [SM, VM, VM, VM, VM],
+                [big, entries, (VM, jax.ShapeDtypeStruct((total, count + LANES), jnp.bfloat16)), wide, wide],
                 scratch_shapes=[pltpu.VMEM((total, LANES), jnp.float32)] * 2,
-            )(rows, rows, stiff, tiled(spring[0]))
-            nearby, base = call(
-                "inner", functools.partial(inner_kernel, chunks), [SM, VM], [big, entries]
-            )(rows, field)
+            )(rows, rows, stiff, tiled(spring[0]), field)
         else:
             field, nearby, base = call(
                 "inner",
                 functools.partial(scatter_inner_kernel, chunks),
-                [SM] + [VM] * 4,
+                [SM] + [VM] * 2,
                 [big, big, entries],
-                input_output_aliases={4: 0},
-            )(rows, entry, *past, nearby)
+                input_output_aliases={2: 0},
+            )(rows, entry, nearby)
+        nearby, base = call(
+            "settle",
+            functools.partial(settle_kernel, chunks),
+            [VM] * 9,
+            [big, entries],
+            input_output_aliases={8: 0},
+        )(got_a, got_b, entry, base, same, weight, factor, stiff, nearby)
         if sweep < ITERS - 1:
             entry, send_x, send_z, halo_a, halo_b = call(
-                "step", functools.partial(step_kernel, chunks), [VM] * 10, [entries, send, send, halo, halo]
-            )(got_x, got_z, got_a, got_b, entry, base, same, weight, factor, stiff)
+                "step", functools.partial(step_kernel, chunks), [VM] * 7, [entries, send, send, halo, halo]
+            )(got_x, got_z, entry, base, same, factor, stiff)
     _, out = call(
         "last",
-        functools.partial(last_kernel, chunks),
-        [SM] + [VM] * 11,
+        last_kernel,
+        [SM] + [VM] * 8,
         [big, (HBM, f32(fields, blocks, LANES))],
         scratch_shapes=[
             pltpu.VMEM((fields, total, LANES), jnp.float32),
             pltpu.SemaphoreType.DMA((2 * LOADS,)),
         ],
         input_output_aliases={1: 0},
-    )(rows, nearby, got_x, got_z, got_a, got_b, entry, base, same, weight, factor, stiff)
+    )(rows, nearby, got_x, got_z, entry, base, same, factor, stiff)
     return untiled(out)[:, None]
 
 

time: 56 us -> 55.1 us (0.984)
  the two profiles are of different devices: /device:TPU:3 before, /device:TPU:0 now
where the time goes in v4:
time: 55.1 us; the launch traced here: 54.8 us
  Pallas kernels  23.4 us (42%)
  starting transfers between devices  16.1 us (29%)
  waiting for transfers between devices  14.3 us (26%)
  other arithmetic  0.71 us (1%)
    ppermute x13, starting transfers between devices, exchange(): return lax.ppermute(array, axis, pairs)  16.1 us
    ppermute x13, waiting for transfers between devices, exchange(): return lax.ppermute(array, axis, pairs)  14.3 us
    pallas_call x2, Pallas kernels, on_device(): call('inner', functools.partial(scatter_inner_kernel, chunks), [SM] + [VM...  8.96 us
    pallas_call x1, Pallas kernels, on_device(): call('start', functools.partial(start_kernel, chunks), [SM, VM, VM, VM, V...  5.08 us
    pallas_call x1, Pallas kernels, on_device(): call('last', last_kernel, [SM] + [VM] * 8, [big, (HBM, f32(fields, blocks...  3.69 us
    pallas_call x1, Pallas kernels, on_device(): call('own', functools.partial(own_kernel, chunks), [VM, HBM], [big, send]...  2.64 us
  transfers between devices with their start and end apart: 13, of which 3 were waited for; matrix products, arithmetic and copies ran while one was open for 0% of the time, Pallas kernels for 32%

profile of v4, /device:TPU:0, one launch (start us, length us, event | category | flops | bytes accessed | tf_op | source)
XLA Modules:
  0.0 54.8 jit_solution(17863525807679090716)
XLA Ops:
  0.0 0.0 copy-start.1
  0.0 0.7 %pad_add_fusion.packed = s32[3,1,256]{2,1,0:T(1,128)S(1)} fusion(s32[1,1,256]{2,1,0:T(1,128)} %bitcast.20, s32[2,1,256]{2,1,0:T(1,128)} %param.8), kind=kLoop, calls=%fused_computation | loop fusion | flops 768 | bytes 6144 | tf_op jit(solution)/shard_map/concatenate | solution.py:413
  0.7 4.9 %collective-permute-start = (s32[3,1,256]{2,1,0:T(1,128)S(1)}, s32[3,1,256]{2,1,0:T(1,128)S(1)}, u32[]{:S(2)}, u32[]{:S(2)}) collective-permute-start(s32[3,1,256]{2,1,0:T(1,128)S(1)} %pad_add_fusion.packed), channel_id=1, source_target_pairs={{0,4},{4,8},{8,12},{12,16},{16,20},{20,24},{24,28},{1,5},{5,9},{9,... | collective-permute-start | bytes 9224 | tf_op jit(solution)/shard_map/ppermute | solution.py:364
  5.6 0.0 copy-start
  5.6 2.6 %own.1 = (f32[2,4096,128]{2,1,0:T(8,128)S(1)}, f32[2,256,128]{2,1,0:T(8,128)S(1)}) custom-call(s32[3,1,256]{2,1,0:T(1,128)S(1)} %pad_add_fusion.packed, f32[2,4096,128]{2,1,0:T(8,128)} %bitcast.19), custom_call_target="tpu_custom_call" | custom-call | tf_op jit(solution)/shard_map/own/pallas_call | solution.py:419
  8.2 0.0 collective-permute-done.prev
  8.2 0.0 copy-done.1
  8.3 1.1 %first.1 = (f32[2,544,128]{2,1,0:T(8,128)S(1)}, f32[512,128]{1,0:T(8,128)S(1)}, s32[1,512]{1,0:T(1,128)S(1)}, f32[2,256,128]{2,1,0:T(8,128)S(1)}, f32[2,256,128]...) custom-call(f32[1,8]{1,0:T(1,128)S(1)} %bitcast.18, s32[3,1,256]{2,1,0:T(1,128)S(1)} %pad_add_fusion.packed, ...), custom_call_target="tpu_custom_call" | custom-call | tf_op jit(solution)/shard_map/first/pallas_call | solution.py:427
  9.3 1.6 %collective-permute-start.1 = (f32[2,256,128]{2,1,0:T(8,128)S(1)}, f32[2,256,128]{2,1,0:T(8,128)S(1)}, u32[]{:S(2)}, u32[]{:S(2)}) collective-permute-start(f32[2,256,128]{2,1,0:T(8,128)S(1)} %get-tuple-element.43), channel_id=1, source_target_pairs={{0,4},{4,0},{8,12},{12,8},{16,20},{20,16},{24,28},{28,24},{1,5},{5... | collective-permute-start | bytes 786440 | tf_op jit(solution)/shard_map/ppermute | solution.py:364
  10.9 0.7 %collective-permute-start.2 = (f32[2,256,128]{2,1,0:T(8,128)S(1)}, f32[2,256,128]{2,1,0:T(8,128)S(1)}, u32[]{:S(2)}, u32[]{:S(2)}) collective-permute-start(f32[2,256,128]{2,1,0:T(8,128)S(1)} %get-tuple-element.44), channel_id=1, source_target_pairs={{4,8},{8,4},{12,16},{16,12},{20,24},{24,20},{5,9},{9,5},{13,17},{1... | collective-permute-start | bytes 786440 | tf_op jit(solution)/shard_map/ppermute | solution.py:364
  11.6 0.1 collective-permute-start.3
  11.7 0.7 %collective-permute-start.4 = (f32[2,16,128]{2,1,0:T(8,128)S(1)}, f32[2,16,128]{2,1,0:T(8,128)S(1)}, u32[]{:S(2)}, u32[]{:S(2)}) collective-permute-start(f32[2,16,128]{2,1,0:T(8,128)S(1)} %get-tuple-element.47), channel_id=1, source_target_pairs={{1,2},{2,1},{5,6},{6,5},{9,10},{10,9},{13,14},{14,13},{17,18},{18,... | collective-permute-start | bytes 49160 | tf_op jit(solution)/shard_map/ppermute | solution.py:364
  12.4 0.0 copy-done
  12.4 5.1 %start.1 = (f32[2,4096,128]{2,1,0:T(8,128)S(1)}, f32[2,544,128]{2,1,0:T(8,128)S(1)}, bf16[544,640]{1,0:T(8,128)(2,1)S(1)}, f32[544,128]{1,0:T(8,128)S(1)}, f32[544,128]{1,0:T(8,128)S(1)}) custom-call(s32[1,512]{1,0:T(1,128)S(1)} %get-tuple-element.42.rows.rows_line, s32[1,512]{1,0:T(1,128)S(1)} %get-tuple-element.42.rows.rows_line, ...), custom_call_target="tpu_custom_call" | custom-call | tf_op jit(solution)/shard_map/start/pallas_call | solution.py:442
  17.5 0.0 collective-permute-done.3.got_a
  17.5 0.0 collective-permute-done.4.got_b
  17.5 0.3 settle.3
  17.8 4.0 %collective-permute-done.1.got_x = f32[2,256,128]{2,1,0:T(8,128)S(1)} collective-permute-done((f32[2,256,128]{2,1,0:T(8,128)S(1)}, f32[2,256,128]{2,1,0:T(8,128)S(1)}, u32[]{:S(2)}, u32[]{:S(2)}) %collective-permute-start.1) | collective-permute-done | bytes 262176 | tf_op jit(solution)/shard_map/ppermute | solution.py:364
  21.9 0.0 collective-permute-done.2.got_z
  21.9 0.5 step.2
  22.4 2.5 %collective-permute-start.5 = (f32[2,256,128]{2,1,0:T(8,128)S(1)}, f32[2,256,128]{2,1,0:T(8,128)S(1)}, u32[]{:S(2)}, u32[]{:S(2)}) collective-permute-start(f32[2,256,128]{2,1,0:T(8,128)S(1)} %get-tuple-element.55), channel_id=1, source_target_pairs={{0,4},{4,0},{8,12},{12,8},{16,20},{20,16},{24,28},{28,24},{1,5},{5... | collective-permute-start | bytes 786440 | tf_op jit(solution)/shard_map/ppermute | solution.py:364
  24.9 0.7 %collective-permute-start.6 = (f32[2,256,128]{2,1,0:T(8,128)S(1)}, f32[2,256,128]{2,1,0:T(8,128)S(1)}, u32[]{:S(2)}, u32[]{:S(2)}) collective-permute-start(f32[2,256,128]{2,1,0:T(8,128)S(1)} %get-tuple-element.56), channel_id=1, source_target_pairs={{4,8},{8,4},{12,16},{16,12},{20,24},{24,20},{5,9},{9,5},{13,17},{1... | collective-permute-start | bytes 786440 | tf_op jit(solution)/shard_map/ppermute | solution.py:364
  25.6 0.4 collective-permute-start.7
  26.0 0.7 %collective-permute-start.8 = (f32[2,16,128]{2,1,0:T(8,128)S(1)}, f32[2,16,128]{2,1,0:T(8,128)S(1)}, u32[]{:S(2)}, u32[]{:S(2)}) collective-permute-start(f32[2,16,128]{2,1,0:T(8,128)S(1)} %get-tuple-element.59), channel_id=1, source_target_pairs={{1,2},{2,1},{5,6},{6,5},{9,10},{10,9},{13,14},{14,13},{17,18},{18,... | collective-permute-start | bytes 49160 | tf_op jit(solution)/shard_map/ppermute | solution.py:364
  26.7 4.5 %inner.2 = (f32[2,4096,128]{2,1,0:T(8,128)S(1)}, f32[2,4096,128]{2,1,0:T(8,128)S(1)}, f32[2,544,128]{2,1,0:T(8,128)S(1)}) custom-call(s32[1,512]{1,0:T(1,128)S(1)} %get-tuple-element.42.rows.rows_line, f32[2,544,128]{2,1,0:T(8,128)S(1)} %get-tuple-element.57.entry.old, f32[2,4096,128]{2,1,0:T(8,128)S(1)} %get-tuple-element.60.stale), custom_call_target="tpu_custom_call", output_to_operand_aliasing={{0}: (2, {})} | custom-call | tf_op jit(solution)/shard_map/inner/pallas_call | solution.py:450
  31.2 0.0 collective-permute-done.7.got_a
  31.2 0.0 collective-permute-done.8.got_b
  31.2 0.3 settle.4
  31.5 5.4 %collective-permute-done.5.got_x = f32[2,256,128]{2,1,0:T(8,128)S(1)} collective-permute-done((f32[2,256,128]{2,1,0:T(8,128)S(1)}, f32[2,256,128]{2,1,0:T(8,128)S(1)}, u32[]{:S(2)}, u32[]{:S(2)}) %collective-permute-start.5) | collective-permute-done | bytes 262176 | tf_op jit(solution)/shard_map/ppermute | solution.py:364
  36.9 0.0 collective-permute-done.6.got_z
  36.9 0.5 step.3
  37.4 2.5 %collective-permute-start.11 = (f32[2,256,128]{2,1,0:T(8,128)S(1)}, f32[2,256,128]{2,1,0:T(8,128)S(1)}, u32[]{:S(2)}, u32[]{:S(2)}) collective-permute-start(f32[2,256,128]{2,1,0:T(8,128)S(1)} %get-tuple-element.71), channel_id=1, source_target_pairs={{0,4},{4,0},{8,12},{12,8},{16,20},{20,16},{24,28},{28,24},{1,5},{5... | collective-permute-start | bytes 786440 | tf_op jit(solution)/shard_map/ppermute | solution.py:364
  40.0 0.7 %collective-permute-start.12 = (f32[2,256,128]{2,1,0:T(8,128)S(1)}, f32[2,256,128]{2,1,0:T(8,128)S(1)}, u32[]{:S(2)}, u32[]{:S(2)}) collective-permute-start(f32[2,256,128]{2,1,0:T(8,128)S(1)} %get-tuple-element.72), channel_id=1, source_target_pairs={{4,8},{8,4},{12,16},{16,12},{20,24},{24,20},{5,9},{9,5},{13,17},{1... | collective-permute-start | bytes 786440 | tf_op jit(solution)/shard_map/ppermute | solution.py:364
  40.7 0.1 collective-permute-start.9
  40.7 0.7 %collective-permute-start.10 = (f32[2,16,128]{2,1,0:T(8,128)S(1)}, f32[2,16,128]{2,1,0:T(8,128)S(1)}, u32[]{:S(2)}, u32[]{:S(2)}) collective-permute-start(f32[2,16,128]{2,1,0:T(8,128)S(1)} %get-tuple-element.65), channel_id=1, source_target_pairs={{1,2},{2,1},{5,6},{6,5},{9,10},{10,9},{13,14},{14,13},{17,18},{18,... | collective-permute-start | bytes 49160 | tf_op jit(solution)/shard_map/ppermute | solution.py:364
  41.4 4.5 %inner.3 = (f32[2,4096,128]{2,1,0:T(8,128)S(1)}, f32[2,4096,128]{2,1,0:T(8,128)S(1)}, f32[2,544,128]{2,1,0:T(8,128)S(1)}) custom-call(s32[1,512]{1,0:T(1,128)S(1)} %get-tuple-element.42.rows.rows_line, f32[2,544,128]{2,1,0:T(8,128)S(1)} %get-tuple-element.66.entry.old, f32[2,4096,128]{2,1,0:T(8,128)S(1)} %get-tuple-element.67.stale), custom_call_target="tpu_custom_call", output_to_operand_aliasing={{0}: (2, {})} | custom-call | tf_op jit(solution)/shard_map/inner/pallas_call | solution.py:450
  45.9 0.0 collective-permute-done.9.got_a
  45.9 0.0 collective-permute-done.10.got_b
  45.9 0.3 settle.5
  46.3 4.9 %collective-permute-done.11.got_x = f32[2,256,128]{2,1,0:T(8,128)S(1)} collective-permute-done((f32[2,256,128]{2,1,0:T(8,128)S(1)}, f32[2,256,128]{2,1,0:T(8,128)S(1)}, u32[]{:S(2)}, u32[]{:S(2)}) %collective-permute-start.11) | collective-permute-done | bytes 262176 | tf_op jit(solution)/shard_map/ppermute | solution.py:364
  51.1 0.0 collective-permute-done.12.got_z
  51.1 3.7 %last.1 = (f32[2,4096,128]{2,1,0:T(8,128)S(1)}, f32[2,4096,128]{2,1,0:T(8,128)}) custom-call(s32[1,512]{1,0:T(1,128)S(1)} %get-tuple-element.42.rows.rows_line, f32[2,4096,128]{2,1,0:T(8,128)S(1)} %get-tuple-element.70.stale, f32[2,256,128]{2,1,0:T(8,128)S(1)} %collective-permute-done.11.got_x, ...), custom_call_target="tpu_custom_call", output_to_operand_aliasing={{0}: (1, {})} | custom-call | tf_op jit(solution)/shard_map/last/pallas_call | solution.py:468
Async XLA Ops:
  0.0 8.2 %copy-start.1 = (f32[8]{0:T(128)S(1)}, f32[8]{0:T(128)}, u32[]{:S(2)}) copy-start(f32[8]{0:T(128)} %param.7) | copy-start | bytes 100
  0.7 7.5 %collective-permute-start = (s32[3,1,256]{2,1,0:T(1,128)S(1)}, s32[3,1,256]{2,1,0:T(1,128)S(1)}, u32[]{:S(2)}, u32[]{:S(2)}) collective-permute-start(s32[3,1,256]{2,1,0:T(1,128)S(1)} %pad_add_fusion.packed), channel_id=1, source_target_pairs={{0,4},{4,8},{8,12},{12,16},{16,20},{20,24},{24,28},{1,5},{5,9},{9,... | collective-permute-start | bytes 9224 | tf_op jit(solution)/shard_map/ppermute | solution.py:364
  5.6 6.8 %copy-start = (f32[1,256,2048]{2,1,0:T(8,128)S(1)}, f32[1,256,2048]{2,1,0:T(8,128)}, u32[]{:S(2)}) copy-start(f32[1,256,2048]{2,1,0:T(8,128)} %param.6) | copy-start | bytes 6291460
  9.3 12.5 %collective-permute-start.1 = (f32[2,256,128]{2,1,0:T(8,128)S(1)}, f32[2,256,128]{2,1,0:T(8,128)S(1)}, u32[]{:S(2)}, u32[]{:S(2)}) collective-permute-start(f32[2,256,128]{2,1,0:T(8,128)S(1)} %get-tuple-element.43), channel_id=1, source_target_pairs={{0,4},{4,0},{8,12},{12,8},{16,20},{20,16},{24,28},{28,24},{1,5},{5... | collective-permute-start | bytes 786440 | tf_op jit(solution)/shard_map/ppermute | solution.py:364
  10.9 10.9 %collective-permute-start.2 = (f32[2,256,128]{2,1,0:T(8,128)S(1)}, f32[2,256,128]{2,1,0:T(8,128)S(1)}, u32[]{:S(2)}, u32[]{:S(2)}) collective-permute-start(f32[2,256,128]{2,1,0:T(8,128)S(1)} %get-tuple-element.44), channel_id=1, source_target_pairs={{4,8},{8,4},{12,16},{16,12},{20,24},{24,20},{5,9},{9,5},{13,17},{1... | collective-permute-start | bytes 786440 | tf_op jit(solution)/shard_map/ppermute | solution.py:364
  11.6 5.8 %collective-permute-start.3 = (f32[2,16,128]{2,1,0:T(8,128)S(1)}, f32[2,16,128]{2,1,0:T(8,128)S(1)}, u32[]{:S(2)}, u32[]{:S(2)}) collective-permute-start(f32[2,16,128]{2,1,0:T(8,128)S(1)} %get-tuple-element.46), channel_id=1, source_target_pairs={{0,1},{1,0},{2,3},{3,2},{4,5},{5,4},{6,7},{7,6},{8,9},{9,8},{10,11... | collective-permute-start | bytes 49160 | tf_op jit(solution)/shard_map/ppermute | solution.py:364
  11.7 5.8 %collective-permute-start.4 = (f32[2,16,128]{2,1,0:T(8,128)S(1)}, f32[2,16,128]{2,1,0:T(8,128)S(1)}, u32[]{:S(2)}, u32[]{:S(2)}) collective-permute-start(f32[2,16,128]{2,1,0:T(8,128)S(1)} %get-tuple-element.47), channel_id=1, source_target_pairs={{1,2},{2,1},{5,6},{6,5},{9,10},{10,9},{13,14},{14,13},{17,18},{18,... | collective-permute-start | bytes 49160 | tf_op jit(solution)/shard_map/ppermute | solution.py:364
  22.4 14.6 %collective-permute-start.5 = (f32[2,256,128]{2,1,0:T(8,128)S(1)}, f32[2,256,128]{2,1,0:T(8,128)S(1)}, u32[]{:S(2)}, u32[]{:S(2)}) collective-permute-start(f32[2,256,128]{2,1,0:T(8,128)S(1)} %get-tuple-element.55), channel_id=1, source_target_pairs={{0,4},{4,0},{8,12},{12,8},{16,20},{20,16},{24,28},{28,24},{1,5},{5... | collective-permute-start | bytes 786440 | tf_op jit(solution)/shard_map/ppermute | solution.py:364
  24.9 12.0 %collective-permute-start.6 = (f32[2,256,128]{2,1,0:T(8,128)S(1)}, f32[2,256,128]{2,1,0:T(8,128)S(1)}, u32[]{:S(2)}, u32[]{:S(2)}) collective-permute-start(f32[2,256,128]{2,1,0:T(8,128)S(1)} %get-tuple-element.56), channel_id=1, source_target_pairs={{4,8},{8,4},{12,16},{16,12},{20,24},{24,20},{5,9},{9,5},{13,17},{1... | collective-permute-start | bytes 786440 | tf_op jit(solution)/shard_map/ppermute | solution.py:364
  25.6 5.6 %collective-permute-start.7 = (f32[2,16,128]{2,1,0:T(8,128)S(1)}, f32[2,16,128]{2,1,0:T(8,128)S(1)}, u32[]{:S(2)}, u32[]{:S(2)}) collective-permute-start(f32[2,16,128]{2,1,0:T(8,128)S(1)} %get-tuple-element.58), channel_id=1, source_target_pairs={{0,1},{1,0},{2,3},{3,2},{4,5},{5,4},{6,7},{7,6},{8,9},{9,8},{10,11... | collective-permute-start | bytes 49160 | tf_op jit(solution)/shard_map/ppermute | solution.py:364
  26.0 5.2 %collective-permute-start.8 = (f32[2,16,128]{2,1,0:T(8,128)S(1)}, f32[2,16,128]{2,1,0:T(8,128)S(1)}, u32[]{:S(2)}, u32[]{:S(2)}) collective-permute-start(f32[2,16,128]{2,1,0:T(8,128)S(1)} %get-tuple-element.59), channel_id=1, source_target_pairs={{1,2},{2,1},{5,6},{6,5},{9,10},{10,9},{13,14},{14,13},{17,18},{18,... | collective-permute-start | bytes 49160 | tf_op jit(solution)/shard_map/ppermute | solution.py:364
  37.4 13.7 %collective-permute-start.11 = (f32[2,256,128]{2,1,0:T(8,128)S(1)}, f32[2,256,128]{2,1,0:T(8,128)S(1)}, u32[]{:S(2)}, u32[]{:S(2)}) collective-permute-start(f32[2,256,128]{2,1,0:T(8,128)S(1)} %get-tuple-element.71), channel_id=1, source_target_pairs={{0,4},{4,0},{8,12},{12,8},{16,20},{20,16},{24,28},{28,24},{1,5},{5... | collective-permute-start | bytes 786440 | tf_op jit(solution)/shard_map/ppermute | solution.py:364
  40.0 11.1 %collective-permute-start.12 = (f32[2,256,128]{2,1,0:T(8,128)S(1)}, f32[2,256,128]{2,1,0:T(8,128)S(1)}, u32[]{:S(2)}, u32[]{:S(2)}) collective-permute-start(f32[2,256,128]{2,1,0:T(8,128)S(1)} %get-tuple-element.72), channel_id=1, source_target_pairs={{4,8},{8,4},{12,16},{16,12},{20,24},{24,20},{5,9},{9,5},{13,17},{1... | collective-permute-start | bytes 786440 | tf_op jit(solution)/shard_map/ppermute | solution.py:364
  40.7 5.2 %collective-permute-start.9 = (f32[2,16,128]{2,1,0:T(8,128)S(1)}, f32[2,16,128]{2,1,0:T(8,128)S(1)}, u32[]{:S(2)}, u32[]{:S(2)}) collective-permute-start(f32[2,16,128]{2,1,0:T(8,128)S(1)} %get-tuple-element.64), channel_id=1, source_target_pairs={{0,1},{1,0},{2,3},{3,2},{4,5},{5,4},{6,7},{7,6},{8,9},{9,8},{10,11... | collective-permute-start | bytes 49160 | tf_op jit(solution)/shard_map/ppermute | solution.py:364
  40.7 5.2 %collective-permute-start.10 = (f32[2,16,128]{2,1,0:T(8,128)S(1)}, f32[2,16,128]{2,1,0:T(8,128)S(1)}, u32[]{:S(2)}, u32[]{:S(2)}) collective-permute-start(f32[2,16,128]{2,1,0:T(8,128)S(1)} %get-tuple-element.65), channel_id=1, source_target_pairs={{1,2},{2,1},{5,6},{6,5},{9,10},{10,9},{13,14},{14,13},{17,18},{18,... | collective-permute-start | bytes 49160 | tf_op jit(solution)/shard_map/ppermute | solution.py:364
